TPU v7x, 128 devices: a whole 4x4x4 slice. The times are simulated.
128 devices in a mesh: wide: 16 (over z_hi, x, core), narrow: 8 (over z_lo, y).
Axes of the slice: x: 4, y: 4, z: 4 (z_hi: 2, z_lo: 2; z = z_hi * 2 + z_lo), core: 2. Of those that a mesh axis runs over, the one named last changes fastest.
Arguments:
- slope_first: float32 [768, 768, 256], P('wide', 'narrow'), may hold values from -3.1416 to 3.1416, as said below
- slope_second: float32 [768, 768, 256], P('wide', 'narrow'), may hold values from -3.1416 to 3.1416, as said below
- slope_third: float32 [768, 768, 256], P('wide', 'narrow'), may hold values from -3.1416 to 3.1416, as said below
Outputs:
- unwrapped_phase: float32 [768, 768, 256], P('wide', 'narrow')
Inputs may be any that keep to these rules, and one draw needn't show every extreme that they name: `slope_first`: wrapped phase differences. `slope_second`: wrapped phase differences. `slope_third`: wrapped phase differences.
All inputs are finite; a program needn't handle non-finite values.
Results may differ from a plain program's by a relative error of at most 0.0003.
Values sent between devices are 32-bit elements; how exact they have to be, the bound alone decides.
A program may use at most 128 MiB of HBM per device.

v0:
```python
import math

import jax
import jax.numpy as jnp
from jax import lax
from jax.sharding import PartitionSpec as P


def passed_along(x, axis, by):
    peers = lax.axis_size(axis)
    pairs = [(i, i + by) for i in range(peers) if 0 <= i + by < peers]
    return lax.ppermute(x, axis, pairs)


def cut_along(x, dim, peers):
    shape = x.shape
    pieces = x.reshape(*shape[:dim], peers, shape[dim] // peers, *shape[dim + 1 :])
    return jnp.moveaxis(pieces, dim, 0)


def cut_rows(length, count):
    step = length // count
    if step >= 8:
        step -= step % 8
    return [step * k for k in range(1, count)]


def in_order(pieces, dim):
    shape = list(pieces.shape[1:])
    shape[dim] *= pieces.shape[0]
    return jnp.moveaxis(pieces, 0, dim).reshape(shape)


def several_exchanges(x, axis, pieces, split_dim, concat_dim):
    blocks = cut_along(x, split_dim, lax.axis_size(axis))
    widest = max(range(1, max(2, blocks.ndim - 1)), key=lambda d: blocks.shape[d])
    outs = []
    for share in jnp.split(blocks, cut_rows(blocks.shape[widest], pieces), axis=widest):
        if share.size:
            outs.append(lax.all_to_all(share, axis, split_axis=0, concat_axis=0, tiled=True))
    return in_order(jnp.concatenate(outs, axis=widest), concat_dim)


def cosine_table(length, columns):
    rows = jnp.arange(length, dtype=jnp.int32)[:, None]
    phase = (2 * columns[None, :] + 1) * rows % (4 * length)
    angle = phase.astype(jnp.float32) * (math.pi / (2 * length))
    weight = jnp.where(rows == 0, math.sqrt(1.0 / length), math.sqrt(2.0 / length))
    return weight * jnp.cos(angle)


def eigen_part(count, index):
    half_sine = jnp.sin(index.astype(jnp.float32) * (math.pi / (2 * count)))
    return -4.0 * half_sine * half_sine


def divide_modes(spectrum, eigenvalue, zero_mode):
    return jnp.where(
        zero_mode, jnp.float32(0.0), spectrum / jnp.where(zero_mode, jnp.float32(1.0), eigenvalue)
    )


def shards(slope_first, slope_second, slope_third):
    rows_local, lines_local, depth = slope_first.shape
    wide_count = lax.axis_size("wide")
    narrow_count = lax.axis_size("narrow")
    wide_place = lax.axis_index("wide")
    narrow_place = lax.axis_index("narrow")
    device_count = wide_count * narrow_count
    device_place = wide_place * narrow_count + narrow_place
    total_first = rows_local * wide_count
    total_second = lines_local * narrow_count
    highest = lax.Precision.HIGHEST
    global_first = wide_place * rows_local + jnp.arange(rows_local, dtype=jnp.int32)
    global_second = narrow_place * lines_local + jnp.arange(lines_local, dtype=jnp.int32)
    depth_index = jnp.arange(depth, dtype=jnp.int32)
    flux_first = jnp.where(
        (global_first < total_first - 1)[:, None, None], slope_first, jnp.float32(0.0)
    )
    flux_second = jnp.where(
        (global_second < total_second - 1)[None, :, None], slope_second, jnp.float32(0.0)
    )
    flux_third = jnp.where((depth_index < depth - 1)[None, None, :], slope_third, jnp.float32(0.0))
    below_first = passed_along(flux_first[-1:], "wide", 1)
    below_second = passed_along(flux_second[:, -1:], "narrow", 1)
    zero_line = jnp.zeros((rows_local, lines_local, 1), jnp.float32)
    source = flux_first - jnp.concatenate([below_first, flux_first[:-1]], axis=0)
    source = source + flux_second - jnp.concatenate([below_second, flux_second[:, :-1]], axis=1)
    source = source + flux_third - jnp.concatenate([zero_line, flux_third[:, :, :-1]], axis=2)
    depth_table = cosine_table(depth, depth_index)
    row_table = cosine_table(total_second, jnp.arange(total_second, dtype=jnp.int32))
    column_table = cosine_table(total_first, jnp.arange(total_first, dtype=jnp.int32))
    freq_first = jnp.arange(total_first, dtype=jnp.int32)
    spectrum = jnp.einsum("abn,kn->kab", source, depth_table, precision=highest)
    spectrum = lax.all_to_all(spectrum, ("wide", "narrow"), split_axis=0, concat_axis=1, tiled=True)
    depth_lines = spectrum.shape[0]
    spectrum = spectrum.reshape(depth_lines, wide_count, narrow_count, rows_local, lines_local)
    column_split = column_table.reshape(total_first, wide_count, rows_local)
    row_split = row_table.reshape(total_second, narrow_count, lines_local)
    spectrum = jnp.einsum("cwnib,kwi->cknb", spectrum, column_split, precision=highest)
    spectrum = jnp.einsum("cknb,qnb->ckq", spectrum, row_split, precision=highest)
    freq_second = jnp.arange(total_second, dtype=jnp.int32)
    freq_third = device_place * depth_lines + jnp.arange(depth_lines, dtype=jnp.int32)
    eigenvalue = (
        eigen_part(depth, freq_third)[:, None, None]
        + eigen_part(total_first, freq_first)[None, :, None]
        + eigen_part(total_second, freq_second)[None, None, :]
    )
    zero_mode = (
        (freq_third == 0)[:, None, None]
        & (freq_first == 0)[None, :, None]
        & (freq_second == 0)[None, None, :]
    )
    solved = divide_modes(spectrum, eigenvalue, zero_mode)
    result = jnp.einsum("ckq,qnb->cknb", solved, row_split, precision=highest)
    result = jnp.einsum("cknb,kwi->cwnib", result, column_split, precision=highest)
    result = result.reshape(depth_lines, device_count * rows_local, lines_local)
    result = several_exchanges(result, ("wide", "narrow"), 2, 1, 0)
    return jnp.einsum("kab,kn->abn", result, depth_table, precision=highest)


def solution(mesh):
    placed = (P("wide", "narrow", None), P("wide", "narrow", None), P("wide", "narrow", None))
    return jax.shard_map(
        shards, mesh=mesh, in_specs=placed, out_specs=P("wide", "narrow", None), check_vma=False
    )
```

profile of v0, /device:TPU:1, one launch (start us, length us, event | category | flops | bytes accessed | tf_op | source)
XLA Modules:
  0.0 336.7 jit_solution(5523703520349274445)
XLA Ops:
  0.0 2.9 broadcast_select_fusion.2
  2.9 0.0 copy-start
  2.9 2.2 copy-done
  5.1 0.0 slice-start.1
  5.1 4.6 %collective-permute-start = (f32[1,96,256]{2,1,0:T(8,128)S(1)}, f32[1,96,256]{2,1,0:T(8,128)S(1)}, u32[]{:S(2)}, u32[]{:S(2)}) collective-permute-start(f32[1,96,256]{2,1,0:T(8,128)S(1)} %slice.20), channel_id=1, source_target_pairs={{0,8},{8,16},{16,24},{24,32},{32,40},{40,48},{48,56},{56,64},{64,7... | collective-permute-start | bytes 294920 | tf_op jit(solution)/shard_map/ppermute | solution.py:12
  9.8 0.0 slice-start.2
  9.8 3.0 broadcast_select_fusion.1
  12.8 0.1 slice.22
  12.9 3.2 collective-permute-start.1
  16.1 0.0 slice-done.1
  16.1 0.0 slice-done.2
  16.1 0.6 broadcast_select_fusion
  16.7 0.0 slice-start
  16.7 0.5 collective-permute-done.1
  17.2 0.0 collective-permute-done
  17.2 1.8 slice-done
  19.0 10.2 %fusion.12 = f32[256,48,96]{0,2,1:T(8,128)} fusion(f32[48,96,256]{2,1,0:T(8,128)S(1)} %broadcast_select_fusion, f32[48,96,256]{2,1,0:T(8,128)S(1)} %broadcast_select_fusion.1, f32[48,96,256]{2,1,0:T(8,128)} %copy-done, f32[47,96,256]{2,1,0:T(8,128)S(1)} %slice-done, f32[1,96,256]{2,1,0:T(8,128)S(1)} %collective-permute-done, ...), kind=kOutput, calls=%fused_computation.15 | convolution fusion | flops 3633119232 | bytes 33013760 | tf_op jit(solution)/shard_map/abn,kn->kab/dot_general | solution.py:94
  29.2 6.3 %copy.13 = f32[256,48,96]{2,1,0:T(8,128)} copy(f32[256,48,96]{0,2,1:T(8,128)} %fusion.12) | data formatting | bytes 9437184 | tf_op jit(solution)/shard_map/abn,kn->kab/dot_general | solution.py:94
  35.5 10.1 %all-to-all-start = ((f32[256,48,96]{2,1,0:T(8,128)}), f32[256,48,96]{2,1,0:T(8,128)}, u32[]{:S(2)}, u32[]{:S(2)}) async-start(f32[256,48,96]{2,1,0:T(8,128)} %copy.13), calls=%async_computation | async-start | bytes 12582912 | tf_op jit(solution)/shard_map/all_to_all | solution.py:95
  45.7 0.1 broadcast_and_fusion
  45.8 0.1 broadcast_add_fusion
  45.9 76.3 %all-to-all-done = f32[256,48,96]{2,1,0:T(8,128)} async-done(((f32[256,48,96]{2,1,0:T(8,128)}), f32[256,48,96]{2,1,0:T(8,128)}, u32[]{:S(2)}, u32[]{:S(2)}) %all-to-all-start) | async-done | bytes 4718624 | tf_op jit(solution)/shard_map/all_to_all | solution.py:95
  122.2 25.5 %fusion = f32[768,2,8,96,1]{0,3,4,2,1:T(8,128)S(1)} fusion(f32[2,16,8,48,96]{4,3,0,2,1:T(8,128)} %bitcast.6, s32[16,48]{1,0:T(8,128)S(1)} %multiply_add_fusion, f32[768]{0:T(1024)S(1)} %get-tuple-element.8), kind=kOutput, calls=%fused_computation.1 | convolution fusion | flops 10877534208 | bytes 9443328 | tf_op jit(solution)/shard_map/cwnib,kwi->cknb/dot_general | solution.py:100
  147.7 22.2 %fusion.19 = f32[2,768,768,1]{2,1,3,0:T(8,128)S(1)} fusion(f32[768,2,8,96,1]{0,3,4,2,1:T(8,128)S(1)} %fusion, s32[8,96]{1,0:T(8,128)S(1)} %multiply_add_fusion.1, f32[768]{0:T(1024)S(1)} %get-tuple-element.8), kind=kOutput, calls=%fused_computation.21 | convolution fusion | flops 10877534208 | bytes 9443328 | tf_op jit(solution)/shard_map/cknb,qnb->ckq/dot_general | solution.py:101
  169.9 21.9 %fusion.6 = f32[2,768,8,96]{1,3,2,0:T(8,128)S(1)} fusion(f32[2,768,768,1]{2,1,3,0:T(8,128)S(1)} %fusion.19, f32[768]{0:T(1024)S(1)} %get-tuple-element.7, f32[2,768]{1,0:T(2,128)S(1)} %broadcast_add_fusion, pred[768]{0:T(1024)(128)(4,1)S(1)} %iota_compare_fusion, pred[2,768]{1,0:T(4,128)(4,1)S(1)} %broadcast_and_fusion, s32[8,96]{1,0:T(8,128)S(1)} %multiply_add_fusion.1, ...), kind=kOutput, calls=%fused_computation.9 | convolution fusion | flops 10883432448 | bytes 9454848 | tf_op jit(solution)/shard_map/ckq,qnb->cknb/dot_general | solution.py:115
  191.8 24.9 %fusion.26 = f32[2,16,8,48,96]{4,3,2,0,1:T(8,128)S(1)} fusion(f32[2,768,8,96]{1,3,2,0:T(8,128)S(1)} %fusion.6, s32[16,48]{1,0:T(8,128)S(1)} %multiply_add_fusion, f32[768]{0:T(1024)S(1)} %get-tuple-element.8), kind=kOutput, calls=%fused_computation.30 | convolution fusion | flops 10877534208 | bytes 9443328 | tf_op jit(solution)/shard_map/cknb,kwi->cwnib/dot_general | solution.py:116
  216.8 0.7 copy.16
  217.4 2.1 fusion.124
  219.5 1.9 copy.17
  221.4 9.9 %all-to-all-start.1 = ((f32[128,2,24,96]{3,2,1,0:T(8,128)}), f32[128,2,24,96]{3,2,1,0:T(8,128)}, u32[]{:S(2)}, u32[]{:S(2)}) async-start(f32[128,2,24,96]{3,2,1,0:T(8,128)} %copy.17), calls=%async_computation.1 | async-start | bytes 6291456 | tf_op jit(solution)/shard_map/all_to_all | solution.py:40
  231.3 2.1 copy.18
  233.4 38.9 %all-to-all-done.1 = f32[128,2,24,96]{3,2,1,0:T(8,128)} async-done(((f32[128,2,24,96]{3,2,1,0:T(8,128)}), f32[128,2,24,96]{3,2,1,0:T(8,128)}, u32[]{:S(2)}, u32[]{:S(2)}) %all-to-all-start.1) | async-done | bytes 2359328 | tf_op jit(solution)/shard_map/all_to_all | solution.py:40
  272.3 46.2 %all_to_all.25 = f32[128,2,24,96]{3,2,1,0:T(8,128)S(1)} all-to-all(f32[128,2,24,96]{3,2,1,0:T(8,128)S(1)} %copy.18), channel_id=1, replica_groups=mesh['wide'=16,'narrow'=8] {'wide','narrow'}, dimensions={0} | all-to-all | bytes 4718592 | tf_op jit(solution)/shard_map/all_to_all | solution.py:40
  318.5 2.8 pad_maximum_fusion
  321.3 15.2 %fusion.2 = f32[48,96,256]{2,1,0:T(8,128)} fusion(f32[256,48,96]{2,1,0:T(8,128)S(1)} %bitcast.54, s32[256]{0:T(256)S(1)} %multiply_add_fusion.2, f32[256]{0:T(256)S(1)} %compare_select_fusion), kind=kOutput, calls=%fused_computation.3 | convolution fusion | flops 3624861696 | bytes 9439232 | tf_op jit(solution)/shard_map/kab,kn->abn/dot_general | solution.py:119
  (13 shorter events, 0.2 us)
Async XLA Ops:
  2.9 2.2 copy-start
  5.1 11.0 %slice-start.1 = ((s8[4718592]{0:T(1024)(128)(4,1)}), s8[524288]{0:T(1024)(128)(4,1)S(1)}, s32[]{:S(2)}) async-start(s8[4718592]{0:T(1024)(128)(4,1)} %bitcast.56), calls=%async_computation.4 | async-start | bytes 1048576
  5.1 12.1 %collective-permute-start = (f32[1,96,256]{2,1,0:T(8,128)S(1)}, f32[1,96,256]{2,1,0:T(8,128)S(1)}, u32[]{:S(2)}, u32[]{:S(2)}) collective-permute-start(f32[1,96,256]{2,1,0:T(8,128)S(1)} %slice.20), channel_id=1, source_target_pairs={{0,8},{8,16},{16,24},{24,32},{32,40},{40,48},{48,56},{56,64},{64,7... | collective-permute-start | bytes 294920 | tf_op jit(solution)/shard_map/ppermute | solution.py:12
  9.8 6.3 %slice-start.2 = ((s8[4718592]{0:T(1024)(128)(4,1)}), s8[4194304]{0:T(1024)(128)(4,1)S(1)}, s32[]{:S(2)}) async-start(s8[4718592]{0:T(1024)(128)(4,1)} %bitcast.56), calls=%async_computation.5 | async-start | bytes 8388608
  12.9 4.4 %collective-permute-start.1 = (f32[48,1,256]{2,1,0:T(1,128)S(1)}, f32[48,1,256]{2,1,0:T(1,128)S(1)}, u32[]{:S(2)}, u32[]{:S(2)}) collective-permute-start(f32[48,1,256]{2,1,0:T(1,128)S(1)} %slice.22), channel_id=1, source_target_pairs={{0,1},{1,2},{2,3},{3,4},{4,5},{5,6},{6,7},{8,9},{9,10},{10,11},{11... | collective-permute-start | bytes 147464 | tf_op jit(solution)/shard_map/ppermute | solution.py:12
  16.7 2.3 slice-start
  35.5 86.8 %all-to-all-start = ((f32[256,48,96]{2,1,0:T(8,128)}), f32[256,48,96]{2,1,0:T(8,128)}, u32[]{:S(2)}, u32[]{:S(2)}) async-start(f32[256,48,96]{2,1,0:T(8,128)} %copy.13), calls=%async_computation | async-start | bytes 12582912 | tf_op jit(solution)/shard_map/all_to_all | solution.py:95
  221.4 50.9 %all-to-all-start.1 = ((f32[128,2,24,96]{3,2,1,0:T(8,128)}), f32[128,2,24,96]{3,2,1,0:T(8,128)}, u32[]{:S(2)}, u32[]{:S(2)}) async-start(f32[128,2,24,96]{3,2,1,0:T(8,128)} %copy.17), calls=%async_computation.1 | async-start | bytes 6291456 | tf_op jit(solution)/shard_map/all_to_all | solution.py:40
where the time goes:
time: 343 us; the launch traced here: 337 us
  matrix products  120 us (35%)
  waiting for transfers between devices  116 us (34%)
  blocking collectives  46.2 us (13%)
  starting transfers between devices  27.8 us (8%)
  local copies, waits for them, and re-layouts  17.1 us (5%)
  other arithmetic  9.51 us (3%)
    all_to_all x1, waiting for transfers between devices, shards(): lax.all_to_all(spectrum, ('wide', 'narrow'), split_axis=0, concat_axis=1,...  76.3 us
    all_to_all x1, blocking collectives, several_exchanges(): lax.all_to_all(share, axis, split_axis=0, concat_axis=0, tiled=True)  46.2 us
    all_to_all x1, waiting for transfers between devices, several_exchanges(): lax.all_to_all(share, axis, split_axis=0, concat_axis=0, tiled=True)  38.9 us
    dot_general x1, matrix products, shards(): jnp.einsum('cwnib,kwi->cknb', spectrum, column_split, precision=highest)  25.5 us
    dot_general x1, matrix products, shards(): jnp.einsum('cknb,kwi->cwnib', result, column_split, precision=highest)  24.9 us
    dot_general x1, matrix products, shards(): jnp.einsum('cknb,qnb->ckq', spectrum, row_split, precision=highest)  22.2 us
    dot_general x1, matrix products, shards(): result = jnp.einsum('ckq,qnb->cknb', solved, row_split, precision=highest)  21.9 us
    dot_general x1, matrix products, shards(): return jnp.einsum('kab,kn->abn', result, depth_table, precision=highest)  15.2 us
  transfers between devices with their start and end apart: 4, of which 3 were waited for; matrix products, arithmetic and copies ran while one was open for 2% of the time, Pallas kernels for 0%

commit v1 on v0

v1 whole, which is shorter than its diff:
```python
import functools
import math

import jax
import jax.numpy as jnp
import numpy as np
from jax import lax
from jax.experimental import pallas as pl
from jax.experimental.pallas import tpu as pltpu
from jax.sharding import PartitionSpec as P

HIGHEST = lax.Precision.HIGHEST


LANES = 128


def cosine_matrix(length):
    k = np.arange(length)[:, None]
    n = np.arange(length)[None, :]
    table = np.sqrt(2.0 / length) * np.cos(np.pi * ((2 * n + 1) * k % (4 * length)) / (2 * length))
    table[0] = np.sqrt(1.0 / length)
    return table


def sine_matrix(parts):
    m = np.arange(1, parts)
    return np.sqrt(2.0 / parts) * np.sin(np.pi * m[:, None] * m[None, :] / parts)


def modes(length):
    return 4.0 * np.sin(np.pi * np.arange(length) / (2 * length)) ** 2


def signs(length):
    return (-1.0) ** np.arange(length)


def face(length):
    return cosine_matrix(length)[:, 0]


def exponent(mu):
    return 2.0 * np.arcsinh(np.sqrt(mu) / 2.0)


def interface_gain(mu, cells, parts):
    kappa = exponent(mu)[..., None]
    angle = np.pi * np.arange(1, parts) / parts
    decay = np.exp(-kappa * cells)
    ratio = -np.expm1(-2.0 * kappa * cells) / (np.expm1(-kappa * cells) ** 2 + 2.0 * decay * (1.0 - np.cos(angle)))
    return np.tanh(kappa / 2.0) * ratio


def running_levels(parts):
    part = np.arange(parts)[:, None]
    step = np.arange(1, parts)[None, :]
    return (step <= part) - (parts - step) / parts


@functools.lru_cache(None)
def tables(rows, lines, depth, wide, narrow):
    t = {}
    row_modes, line_modes, depth_modes = modes(rows), modes(lines), modes(depth)
    row_face, line_face = face(rows), face(lines)
    sine_n = sine_matrix(narrow)
    gain = interface_gain(depth_modes[:, None] + row_modes[None, :], lines, narrow)
    gain[0, 0, :] = 0.0
    t["narrow_gain"] = np.swapaxes(gain, 1, 2)
    t["narrow_sines"] = np.einsum("jm,ml->mjl", sine_n, sine_n)
    levels_n = running_levels(narrow)
    t["narrow_steady"] = np.cumsum(-levels_n / line_face[0], axis=0)[:-1] / line_face[0]
    full = cosine_matrix(lines * narrow)
    local = cosine_matrix(lines)
    t["join"] = np.einsum("qJn,kn->qJk", full.reshape(lines * narrow, narrow, lines), local).reshape(
        lines * narrow, lines * narrow
    )
    t["wide_decay"] = np.expm1(-exponent(depth_modes[:, None] + modes(lines * narrow)[None, :]) * rows)
    t["wide_sine"] = sine_matrix(wide)
    t["wide_angle"] = 1.0 - np.cos(np.pi * np.arange(1, wide) / wide)
    t["wide_levels"] = -running_levels(wide) / (row_face[0] * math.sqrt(narrow))
    balance = -(row_face[0] / line_face[0]) * np.tril(np.ones((narrow - 1, narrow)))
    t["balance"] = balance.T
    k = np.arange(1, lines)
    near = np.sum(line_face[k] ** 2 / line_modes[k])
    far = np.sum(signs(lines)[k] * line_face[k] ** 2 / line_modes[k])
    link = (1.0 + 2.0 * near) * np.eye(narrow - 1) - far * (np.eye(narrow - 1, k=1) + np.eye(narrow - 1, k=-1))
    t["level_of_flux"] = (levels_n @ link / line_face[0]).T
    t["level_of_jump"] = (-levels_n / line_face[0]).T
    return {name: np.ascontiguousarray(value, dtype=np.float32) for name, value in t.items()}


def halves(table):
    table = np.asarray(table, np.float32)
    high = table.astype(jnp.bfloat16)
    low = (table - high.astype(np.float32)).astype(jnp.bfloat16)
    return high, low


def left_table(table):
    high, low = halves(table)
    return np.block([[high, high], [low, np.zeros_like(low)]])


def split(x):
    high = x.astype(jnp.bfloat16)
    return high, (x - high.astype(jnp.float32)).astype(jnp.bfloat16)


def dot(a, b):
    return jnp.dot(a, b, preferred_element_type=jnp.float32)


def from_left(table, x):
    both = dot(table, jnp.concatenate(split(x), axis=0))
    count = x.shape[0]
    return both[:count] + both[count:]


def from_right(x, high_table, low_table):
    high, low = split(x)
    return dot(high, high_table) + dot(low, high_table) + dot(high, low_table)


def lower_neighbour(x, axis):
    index = lax.broadcasted_iota(jnp.int32, x.shape, axis)
    x = jnp.where(index < x.shape[axis] - 1, x, 0.0)
    return pltpu.roll(x, 1, axis) - x


def put(held, where, value):
    for panel in range(held.shape[0]):
        held[panel, where, :] = value[:, panel * LANES : (panel + 1) * LANES]


def take(held, where):
    return jnp.concatenate([held[panel, where, :] for panel in range(held.shape[0])], axis=1)


def forward_kernel(
    steps,
    first_ref,
    second_ref,
    third_ref,
    depth_high_ref,
    depth_low_ref,
    line_ref,
    row_ref,
    shift_ref,
    faces_ref,
    line_shift_ref,
    line_face_ref,
    out_ref,
    wide_ref,
    narrow_ref,
    carry,
    held,
):
    step = pl.program_id(0)
    rows, lines = row_ref.shape[0] // 2, line_ref.shape[0] // 2
    block = first_ref.shape[0]
    group = out_ref.shape[0]

    @pl.when(step == 0)
    def _():
        carry[...] = jnp.zeros_like(carry)
        narrow_ref[...] = jnp.zeros_like(narrow_ref)

    @pl.when(step < steps)
    def _():
        below = carry[...]
        parts = []
        for i in range(block):
            here = first_ref[i]
            if i == block - 1:
                here = jnp.where(step < steps - 1, here, 0.0)
            part = below - here + lower_neighbour(second_ref[i], 0) + lower_neighbour(third_ref[i], 1)
            below = here
            parts.append(part)
        carry[...] = below
        stacked = from_right(jnp.concatenate(parts, axis=0), depth_high_ref[...], depth_low_ref[...])
        for i in range(block):
            part = from_left(line_ref[...], stacked[i * lines : (i + 1) * lines])
            put(held, pl.ds(pl.multiple_of((step * block + i) * lines, 8), lines), part)

    @pl.when(step >= steps)
    def _():
        lows, highs = [], []
        narrow_low, narrow_high = narrow_ref[0], narrow_ref[1]
        for i in range(group):
            line = (step - steps) * group + i
            part = from_left(row_ref[...], take(held, pl.ds(line, rows, stride=lines)))
            out_ref[i] = part
            eig = shift_ref[...] + line_shift_ref[line]
            good = eig > 0.0
            closed = jnp.where(good, part / jnp.where(good, eig, 1.0), 0.0)
            lows.append(jnp.sum(closed * faces_ref[0], axis=0, keepdims=True))
            highs.append(jnp.sum(closed * faces_ref[1], axis=0, keepdims=True))
            closed = closed * line_face_ref[line]
            narrow_low = narrow_low + closed
            narrow_high = narrow_high + closed if i % 2 == 0 else narrow_high - closed
        wide_ref[0] = jnp.concatenate(lows, axis=0)
        wide_ref[1] = jnp.concatenate(highs, axis=0)
        narrow_ref[0] = narrow_low
        narrow_ref[1] = narrow_high


def inverse_kernel(
    steps,
    spectrum_ref,
    wide_ref,
    narrow_ref,
    level_ref,
    depth_high_ref,
    depth_low_ref,
    line_ref,
    row_ref,
    shift_ref,
    faces_ref,
    line_shift_ref,
    line_face_ref,
    out_ref,
    held,
):
    step = pl.program_id(0)
    rows, lines = row_ref.shape[0] // 2, line_ref.shape[0] // 2
    block = out_ref.shape[0]
    group = spectrum_ref.shape[0]

    @pl.when(step < steps)
    def _():
        for i in range(group):
            line = step * group + i
            added = faces_ref[1] * wide_ref[1, i : i + 1, :] - faces_ref[0] * wide_ref[0, i : i + 1, :]
            turned = narrow_ref[1] if i % 2 == 0 else -narrow_ref[1]
            part = spectrum_ref[i] + added + line_face_ref[line] * (turned - narrow_ref[0])
            eig = shift_ref[...] + line_shift_ref[line]
            good = eig > 0.0
            part = jnp.where(good, part / jnp.where(good, eig, 1.0), level_ref[...])
            put(held, pl.ds(line, rows, stride=lines), from_left(row_ref[...], part))

    @pl.when(step >= steps)
    def _():
        parts = []
        for i in range(block):
            here = pl.multiple_of(((step - steps) * block + i) * lines, 8)
            parts.append(from_left(line_ref[...], take(held, pl.ds(here, lines))))
        result = from_right(jnp.concatenate(parts, axis=0), depth_high_ref[...], depth_low_ref[...])
        for i in range(block):
            out_ref[i] = result[i * lines : (i + 1) * lines]


BLOCK = 4
GROUP = 8


def box_tables(rows, lines, depth):
    shift = modes(rows)[:, None] + modes(depth)[None, :]
    low = np.broadcast_to(face(rows)[:, None], (rows, depth))
    high = np.broadcast_to((face(rows) * signs(rows))[:, None], (rows, depth))
    faces = np.stack([low, high])
    return [jnp.asarray(v, jnp.float32) for v in (shift, faces, modes(lines), face(lines))]


def whole(*shape):
    return pl.BlockSpec(shape, lambda s: (0,) * len(shape))


def table_specs(rows, lines, depth):
    return [
        whole(depth, depth),
        whole(depth, depth),
        whole(2 * lines, 2 * lines),
        whole(2 * rows, 2 * rows),
        whole(rows, depth),
        whole(2, rows, depth),
        pl.BlockSpec(memory_space=pltpu.SMEM),
        pl.BlockSpec(memory_space=pltpu.SMEM),
    ]


def forward(first, second, third):
    rows, lines, depth = first.shape
    steps, groups = rows // BLOCK, lines // GROUP
    slab = pl.BlockSpec((BLOCK, lines, depth), lambda s: (jnp.minimum(s, steps - 1), 0, 0))
    depth_high, depth_low = halves(cosine_matrix(depth).T)
    f32 = jnp.float32
    return pl.pallas_call(
        functools.partial(forward_kernel, steps),
        grid=(steps + groups,),
        out_shape=[
            jax.ShapeDtypeStruct((lines, rows, depth), f32),
            jax.ShapeDtypeStruct((2, lines, depth), f32),
            jax.ShapeDtypeStruct((2, rows, depth), f32),
        ],
        in_specs=[slab, slab, slab] + table_specs(rows, lines, depth),
        out_specs=[
            pl.BlockSpec((GROUP, rows, depth), lambda s: (jnp.maximum(s - steps, 0), 0, 0)),
            pl.BlockSpec((2, GROUP, depth), lambda s: (0, jnp.maximum(s - steps, 0), 0)),
            whole(2, rows, depth),
        ],
        scratch_shapes=[pltpu.VMEM((lines, depth), f32), pltpu.VMEM((depth // LANES, rows * lines, LANES), f32)],
        compiler_params=pltpu.CompilerParams(vmem_limit_bytes=48 * 2**20),
    )(
        first,
        second,
        third,
        jnp.asarray(depth_high),
        jnp.asarray(depth_low),
        jnp.asarray(left_table(cosine_matrix(lines))),
        jnp.asarray(left_table(cosine_matrix(rows))),
        *box_tables(rows, lines, depth),
    )


def inverse(spectrum, wide_flux, narrow_flux, level):
    lines, rows, depth = spectrum.shape
    steps, groups = rows // BLOCK, lines // GROUP
    depth_high, depth_low = halves(cosine_matrix(depth))
    return pl.pallas_call(
        functools.partial(inverse_kernel, groups),
        grid=(steps + groups,),
        out_shape=jax.ShapeDtypeStruct((rows, lines, depth), jnp.float32),
        in_specs=[
            pl.BlockSpec((GROUP, rows, depth), lambda s: (jnp.minimum(s, groups - 1), 0, 0)),
            pl.BlockSpec((2, GROUP, depth), lambda s: (0, jnp.minimum(s, groups - 1), 0)),
            whole(2, rows, depth),
            whole(1, depth),
        ]
        + table_specs(rows, lines, depth),
        out_specs=pl.BlockSpec((BLOCK, lines, depth), lambda s: (jnp.maximum(s - groups, 0), 0, 0)),
        scratch_shapes=[pltpu.VMEM((depth // LANES, rows * lines, LANES), jnp.float32)],
        compiler_params=pltpu.CompilerParams(vmem_limit_bytes=48 * 2**20),
    )(
        spectrum,
        wide_flux,
        narrow_flux,
        level,
        jnp.asarray(depth_high),
        jnp.asarray(depth_low),
        jnp.asarray(left_table(cosine_matrix(lines).T)),
        jnp.asarray(left_table(cosine_matrix(rows).T)),
        *box_tables(rows, lines, depth),
    )


def own(table, place, count):
    return lax.dynamic_slice_in_dim(jnp.asarray(table), place * count, count, axis=0)


def alternate(length):
    return jnp.asarray(signs(length), jnp.float32)


def eigen(index, count):
    half_sine = jnp.sin(index.astype(jnp.float32) * (math.pi / (2 * count)))
    return 4.0 * half_sine * half_sine


def interfaces(traces, t, place, rows, lines, depth, wide, narrow):
    count = traces.shape[1]
    traces = traces.reshape(wide, narrow, count, -1)
    traces = jnp.transpose(traces, (2, 0, 1, 3))
    cut = [lines, 2 * lines, 2 * lines + rows]
    wide_low, wide_high, narrow_low, narrow_high = jnp.split(traces, cut, axis=-1)
    jump_wide = wide_low[:, 1:] - wide_high[:, :-1]
    jump_narrow = narrow_low[:, :, 1:] - narrow_high[:, :, :-1]
    depth_place = place * count + jnp.arange(count)
    steady = depth_place == 0
    depth_part = eigen(depth_place, depth)
    row_zero = jnp.arange(rows) == 0
    line_zero = jnp.arange(lines) == 0
    last = jnp.einsum("mjl,rmk->rjlk", t["narrow_sines"], own(t["narrow_gain"], place, count), precision=HIGHEST)
    first = jnp.where(
        steady[:, None, None, None] & row_zero, jnp.asarray(t["narrow_steady"])[None, :, :, None], last
    )
    eig = (
        depth_part[:, None, None]
        + jnp.asarray(modes(rows), jnp.float32)[:, None]
        + jnp.asarray(modes(lines), jnp.float32)[None, :]
    )
    faces = jnp.asarray(face(rows)[:, None] * face(lines)[None, :], jnp.float32)
    steady_row = steady[:, None, None] & row_zero[:, None]
    zero_mode = steady_row & line_zero
    weight = faces / jnp.where(zero_mode, 1.0, eig)
    weight_first = jnp.where(steady_row & ~line_zero, 0.0, weight)
    weight_last = jnp.swapaxes(jnp.where(zero_mode, 0.0, weight), 1, 2)
    to_wide = jnp.stack([weight_first, weight_first * alternate(rows)[:, None]], axis=2)
    to_narrow = jnp.stack([weight_last, weight_last * alternate(lines)[:, None]], axis=2)
    shift = depth_part[:, None] + jnp.asarray(modes(lines * narrow), jnp.float32)[None, :]
    decay = own(t["wide_decay"], place, count)
    top = -jnp.sqrt(shift / (4.0 + shift)) * decay * (2.0 + decay)
    top = top[:, None, :]
    decay = decay[:, None, :]
    bottom = decay * decay + 2.0 * (1.0 + decay) * jnp.asarray(t["wide_angle"])[None, :, None]
    wide_gain = top / bottom
    flux = jnp.sum(first[:, None] * jump_narrow[:, :, None], axis=3)
    moved = jnp.einsum("rIjk,rksb->rsIjb", flux, to_wide, precision=HIGHEST)
    edge = [(0, 0)] * 3
    moved = jnp.pad(moved, edge + [(0, 1), (0, 0)]) * alternate(lines) - jnp.pad(moved, edge + [(1, 0), (0, 0)])
    jump_wide = jump_wide + moved[:, 0, 1:] - moved[:, 1, :-1]
    jump_wide = jump_wide.reshape(count, wide - 1, narrow * lines)
    joined = jnp.einsum("riy,qy->riq", jump_wide, t["join"], precision=HIGHEST)
    shaped = jnp.einsum("mi,riq->rmq", t["wide_sine"], joined, precision=HIGHEST)
    shaped = shaped * wide_gain
    shaped = jnp.einsum("mi,rmq->riq", t["wide_sine"], shaped, precision=HIGHEST)
    flux_wide = jnp.einsum("riq,qy->riy", shaped, t["join"], precision=HIGHEST)
    flux_wide = flux_wide.reshape(count, wide - 1, narrow, lines)
    flux_wide = jnp.pad(flux_wide, [(0, 0), (1, 1), (0, 0), (0, 0)])
    moved = jnp.einsum("riJb,rbsk->rsiJk", flux_wide, to_narrow, precision=HIGHEST)
    moved = moved[:, :, 1:] * alternate(rows) - moved[:, :, :-1]
    jump_narrow = jump_narrow + moved[:, 0, :, 1:] - moved[:, 1, :, :-1]
    flux_narrow = jnp.sum(last[:, None] * jump_narrow[:, :, None], axis=3)
    mean_flux = flux_wide[0, 1:, :, 0] - flux_wide[0, :-1, :, 0]
    balanced = jnp.einsum("IJ,Jj->Ij", mean_flux, t["balance"], precision=HIGHEST)
    level = jnp.einsum("Ij,jJ->IJ", balanced, t["level_of_flux"], precision=HIGHEST)
    level = level + jnp.einsum("Ij,jJ->IJ", jump_narrow[0, :, :, 0], t["level_of_jump"], precision=HIGHEST)
    level = level + jnp.einsum("Ii,i->I", t["wide_levels"], joined[0, :, 0], precision=HIGHEST)[:, None]
    flux_narrow = jnp.where(
        steady[:, None, None, None] & row_zero, balanced[None, :, :, None], flux_narrow
    )
    flux_narrow = jnp.pad(flux_narrow, [(0, 0), (0, 0), (1, 1), (0, 0)])
    level = jnp.broadcast_to(level[None, :, :, None], (count, wide, narrow, 8))
    out = jnp.concatenate(
        [flux_wide[:, :-1], flux_wide[:, 1:], flux_narrow[:, :, :-1], flux_narrow[:, :, 1:], level], axis=-1
    )
    out = jnp.transpose(out, (1, 2, 0, 3))
    return out.reshape(wide * narrow, count, -1)


def shards(slope_first, slope_second, slope_third):
    rows, lines, depth = slope_first.shape
    wide = lax.axis_size("wide")
    narrow = lax.axis_size("narrow")
    wide_place = lax.axis_index("wide")
    narrow_place = lax.axis_index("narrow")
    place = wide_place * narrow + narrow_place
    devices = wide * narrow
    t = tables(rows, lines, depth, wide, narrow)
    row_table = jnp.asarray(cosine_matrix(rows), jnp.float32)
    line_table = jnp.asarray(cosine_matrix(lines), jnp.float32)
    depth_table = jnp.asarray(cosine_matrix(depth), jnp.float32)
    spectrum, wide_traces, narrow_traces = forward(slope_first, slope_second, slope_third)
    slope_wide = jnp.einsum("yz,rz->yr", slope_first[-1], depth_table, precision=HIGHEST)
    slope_wide = jnp.einsum("yr,ky->kr", slope_wide, line_table, precision=HIGHEST)
    slope_narrow = jnp.einsum("xz,rz->xr", slope_second[:, -1], depth_table, precision=HIGHEST)
    slope_narrow = jnp.einsum("xr,kx->kr", slope_narrow, row_table, precision=HIGHEST)
    traces = jnp.concatenate(
        [wide_traces[0], wide_traces[1] + slope_wide, narrow_traces[0], narrow_traces[1] + slope_narrow], axis=0
    )
    traces = jnp.transpose(traces).reshape(devices, depth // devices, -1)
    traces = lax.all_to_all(traces, ("wide", "narrow"), split_axis=0, concat_axis=0, tiled=True)
    fluxes = interfaces(traces, t, place, rows, lines, depth, wide, narrow)
    fluxes = lax.all_to_all(fluxes, ("wide", "narrow"), split_axis=0, concat_axis=0, tiled=True)
    fluxes = jnp.transpose(fluxes.reshape(depth, -1))
    wide_flux = fluxes[: 2 * lines].reshape(2, lines, depth)
    narrow_flux = fluxes[2 * lines : 2 * (lines + rows)].reshape(2, rows, depth)
    level = fluxes[2 * (lines + rows) :][:1]
    return inverse(spectrum, wide_flux, narrow_flux, level)


def solution(mesh):
    placed = P("wide", "narrow", None)
    return jax.shard_map(shards, mesh=mesh, in_specs=(placed, placed, placed), out_specs=placed, check_vma=False)
```

time: 343 us -> 102 us (0.30); the launches traced: 337 us -> 101 us
  matrix products: 120 us -> 9.71 us
  waiting for transfers between devices: 116 us -> 10 us
  Pallas kernels: 0 us -> 36 us
  blocking collectives: 46.2 us -> 16.4 us
  starting transfers between devices: 27.8 us -> 11.5 us
  other arithmetic: 9.51 us -> 2.04 us
    dot_general x6 -> x15, matrix products: 120 us -> 9.71 us  [the longest x1 2.23 us: interfaces(): joined = jnp.einsum('riy,qy->riq', jump_wide, t['join'], precision=HIGHEST)]
    all_to_all x2 -> x1, waiting for transfers between devices: 115 us -> 10 us  [shards(): lax.all_to_all(traces, ('wide', 'narrow'), split_axis=0, concat_axis=0, t...]
    pallas_call x0 -> x2, Pallas kernels: none -> 36 us  [the longest x1 19.8 us: forward(): pl.pallas_call(functools.partial(forward_kernel, steps), grid=(steps + gr...]
    all_to_all x1, blocking collectives: 46.2 us -> 16.4 us  [shards(): lax.all_to_all(fluxes, ('wide', 'narrow'), split_axis=0, concat_axis=0, t...]
    unnamed x6 -> x70, local copies, waits for them, and re-layouts: 2.19 us -> 11.1 us
    all_to_all x2 -> x1, starting transfers between devices: 20 us -> 11.5 us  [shards(): lax.all_to_all(traces, ('wide', 'narrow'), split_axis=0, concat_axis=0, t...]
    ppermute x2 -> x0, starting transfers between devices: 7.84 us -> none  [passed_along(): return lax.ppermute(x, axis, pairs)]
    dot_general x1 -> x0, local copies, waits for them, and re-layouts: 6.28 us -> none  [shards(): spectrum = jnp.einsum('abn,kn->kab', source, depth_table, precision=highest)]
  transfers between devices with their start and end apart: 4 -> 1, of which waited for: 3 -> 1; matrix products, arithmetic and copies ran while one was open for 2% -> 2% of each run, Pallas kernels for 0% -> 0%
where the time goes in v1:
time: 102 us; the launch traced here: 101 us
  Pallas kernels  36 us (35%)
  blocking collectives  16.4 us (16%)
  local copies, waits for them, and re-layouts  15.1 us (15%)
  starting transfers between devices  11.5 us (11%)
  waiting for transfers between devices  10 us (10%)
  matrix products  9.71 us (10%)
  other arithmetic  2.04 us (2%)
    pallas_call x1, Pallas kernels, forward(): pl.pallas_call(functools.partial(forward_kernel, steps), grid=(steps + gr...  19.8 us
    all_to_all x1, blocking collectives, shards(): lax.all_to_all(fluxes, ('wide', 'narrow'), split_axis=0, concat_axis=0, t...  16.4 us
    pallas_call x1, Pallas kernels, inverse(): pl.pallas_call(functools.partial(inverse_kernel, groups), grid=(steps + g...  16.2 us
    all_to_all x1, starting transfers between devices, shards(): lax.all_to_all(traces, ('wide', 'narrow'), split_axis=0, concat_axis=0, t...  11.5 us
    unnamed x70, local copies, waits for them, and re-layouts  11.1 us
    all_to_all x1, waiting for transfers between devices, shards(): lax.all_to_all(traces, ('wide', 'narrow'), split_axis=0, concat_axis=0, t...  10 us
    dot_general x1, matrix products, interfaces(): joined = jnp.einsum('riy,qy->riq', jump_wide, t['join'], precision=HIGHEST)  2.23 us
  transfers between devices with their start and end apart: 1, of which 1 were waited for; matrix products, arithmetic and copies ran while one was open for 2% of the time, Pallas kernels for 0%

profile of v1, /device:TPU:1, one launch (start us, length us, event | category | flops | bytes accessed | tf_op | source)
XLA Modules:
  0.0 101.5 jit_solution(5829445524946464272)
XLA Ops:
  0.0 1.0 %slice.92 = f32[48,1,256]{2,1,0:T(1,128)S(1)} slice(f32[48,96,256]{2,1,0:T(8,128)} %second_ref.1), slice={[0:48], [95:96], [0:256]} | slice | bytes 98304 | tf_op jit(solution)/shard_map/slice | solution.py:446
  1.0 1.3 %fusion.16 = f32[256,48]{0,1:T(8,128)S(1)} fusion(f32[256,256]{1,0:T(8,128)} %constant.98.clone, f32[48,1,256]{2,1,0:T(1,128)S(1)} %slice.92), kind=kOutput, calls=%fused_computation.54 | convolution fusion | flops 37748736 | bytes 360448 | tf_op jit(solution)/shard_map/xz,rz->xr/dot_general | solution.py:446
  2.4 1.4 %fusion.9 = f32[256,96]{0,1:T(8,128)S(1)} fusion(f32[256,256]{1,0:T(8,128)} %constant.98.clone, f32[48,96,256]{2,1,0:T(8,128)} %first_ref.1), kind=kOutput, calls=%fused_computation.41 | convolution fusion | flops 75497472 | bytes 458752 | tf_op jit(solution)/shard_map/yz,rz->yr/dot_general | solution.py:444
  3.7 0.9 copy-done.2
  4.6 0.8 copy-done.4
  5.4 0.9 copy-done.8
  6.3 0.9 copy-done.9
  7.2 0.9 copy-done.11
  8.1 0.7 copy-done.13
  8.9 0.7 copy-done.14
  9.5 0.7 copy-done.16
  10.3 19.8 %shard_map.397 = (f32[96,48,256]{2,1,0:T(8,128)S(1)}, f32[2,96,256]{2,1,0:T(8,128)S(1)}, f32[2,48,256]{2,1,0:T(8,128)S(1)}) custom-call(f32[48,96,256]{2,1,0:T(8,128)} %first_ref.1, f32[48,96,256]{2,1,0:T(8,128)} %second_ref.1, f32[48,96,256]{2,1,0:T(8,128)} %third_ref.1, bf16[256,256]{1,0:T(8,128)(2,1)S(1)} %copy-done.9, bf16[256,256]{1,0:T(8,128)(2,1)S(1)} %copy-done.8, ...), custom_call_target="tpu_custom_call" | custom-call | tf_op jit(solution)/shard_map/pallas_call | solution.py:288
  30.1 2.2 %copy-done = f32[96,48,256]{2,1,0:T(8,128)} copy-done((f32[96,48,256]{2,1,0:T(8,128)}, f32[96,48,256]{2,1,0:T(8,128)S(1)}, u32[]{:S(2)}) %copy-start) | copy-done | bytes 4718616
  32.3 0.2 convolution_add_fusion
  32.6 0.2 convolution_add_fusion.1
  32.8 0.2 copy.81
  33.0 1.0 reshape.225
  34.0 11.5 %all-to-all-start = ((f32[128,2,288]{2,1,0:T(2,128)}), f32[128,2,288]{2,1,0:T(2,128)S(1)}, u32[]{:S(2)}, u32[]{:S(2)}) async-start(f32[128,2,288]{2,1,0:T(2,128)} %reshape.225), calls=%async_computation | async-start | bytes 786432 | tf_op jit(solution)/shard_map/all_to_all | solution.py:452
  45.7 0.1 and_select_fusion
  45.9 0.1 divide_select_fusion
  46.0 0.8 fusion.21
  46.8 0.9 broadcast_select_fusion.1
  47.7 10.0 %all-to-all-done = f32[128,2,288]{2,1,0:T(2,128)S(1)} async-done(((f32[128,2,288]{2,1,0:T(2,128)}), f32[128,2,288]{2,1,0:T(2,128)S(1)}, u32[]{:S(2)}, u32[]{:S(2)}) %all-to-all-start) | async-done | bytes 294944 | tf_op jit(solution)/shard_map/all_to_all | solution.py:452
  57.7 0.1 copy.115
  57.9 0.1 slice_subtract_fusion.2
  58.1 0.3 convolution_bitcast_fusion.1
  58.5 0.1 fusion.2
  58.6 0.1 reshape.244
  58.8 2.2 %fusion.29 = f32[2,15,768]{2,1,0:T(8,128)S(1)} fusion(f32[2,15,768]{2,1,0:T(8,128)S(1)} %reshape.244, f32[768,768,1]{1,0,2:T(8,128)S(1)} %copy-done.18), kind=kOutput, calls=%fused_computation.84 | convolution fusion | flops 212336640 | bytes 2543616 | tf_op jit(solution)/shard_map/riy,qy->riq/dot_general | solution.py:403
  61.0 0.1 slice_reduce_fusion.1
  61.1 0.2 fusion
  61.4 0.3 convolution_bitcast_fusion.2
  61.7 1.5 %fusion.30 = f32[2,15,768]{2,1,0:T(8,128)S(1)} fusion(f32[2,15,768]{2,1,0:T(8,128)S(1)} %convolution_bitcast_fusion.2, f32[768,768,1]{1,0,2:T(8,128)S(1)} %copy-done.18), kind=kOutput, calls=%fused_computation.85 | convolution fusion | flops 212336640 | bytes 2543616 | tf_op jit(solution)/shard_map/riq,qy->riy/dot_general | solution.py:407
  63.1 0.1 reshape.245
  63.5 0.5 convolution_bitcast_fusion
  64.1 0.1 fusion.4
  64.4 0.2 fusion.31
  64.6 0.2 fusion.32
  64.9 0.1 convolution_bitcast_fusion.5
  65.0 0.2 fusion.1
  65.3 0.2 concatenate.7
  65.6 0.1 copy.116
  65.7 0.3 copy.92
  66.0 16.4 %all_to_all.10 = f32[128,2,296]{2,1,0:T(2,128)S(1)} all-to-all(f32[128,2,296]{2,1,0:T(2,128)S(1)} %copy.92), channel_id=1, replica_groups=mesh['wide'=16,'narrow'=8] {'wide','narrow'}, dimensions={0} | all-to-all | bytes 606208 | tf_op jit(solution)/shard_map/all_to_all | solution.py:454
  82.4 0.3 reshape.230
  82.7 0.1 copy.93
  83.0 2.3 %copy-done.1 = f32[96,48,256]{2,1,0:T(8,128)S(1)} copy-done((f32[96,48,256]{2,1,0:T(8,128)S(1)}, f32[96,48,256]{2,1,0:T(8,128)}, u32[]{:S(2)}) %copy-start.1) | copy-done | bytes 4718616
  85.3 16.2 %shard_map.398 = f32[48,96,256]{2,1,0:T(8,128)} custom-call(f32[96,48,256]{2,1,0:T(8,128)S(1)} %copy-done.1, f32[2,96,256]{2,1,0:T(8,128)S(1)} %bitcast.118, f32[2,48,256]{2,1,0:T(8,128)S(1)} %bitcast.119, f32[1,256]{1,0:T(1,128)S(1)} %slice.128.level_ref, bf16[256,256]{1,0:T(8,128)(2,1)S(1)} %copy-done.7, bf16[256,256]{1,0:T(8,128)(2,1)S(1)} %copy-done.6, ...), custom_call_target="tpu_custom_call" | custom-call | tf_op jit(solution)/shard_map/pallas_call | solution.py:320
  (84 shorter events, 1.2 us)
Async XLA Ops:
  3.7 0.9 copy-start.2
  4.6 0.8 copy-start.4
  5.4 0.9 copy-start.8
  6.3 0.9 copy-start.9
  7.2 0.9 copy-start.11
  8.1 0.7 copy-start.13
  8.9 0.7 copy-start.14
  9.5 0.7 copy-start.16
  10.2 22.1 %copy-start.19 = (f32[96,96]{1,0:T(8,128)S(1)}, f32[96,96]{1,0:T(8,128)}, u32[]{:S(2)}) copy-start(f32[96,96]{1,0:T(8,128)} %constant.42.clone) | copy-start | bytes 110596
  10.2 22.4 %copy-start.23 = (f32[48,48]{1,0:T(8,128)S(1)}, f32[48,48]{1,0:T(8,128)}, u32[]{:S(2)}) copy-start(f32[48,48]{1,0:T(8,128)} %constant.41.clone) | copy-start | bytes 27652
  10.2 35.5 %copy-start.30 = (f32[48]{0:T(128)S(1)}, f32[48]{0:T(128)}, u32[]{:S(2)}) copy-start(f32[48]{0:T(128)} %constant.110.clone) | copy-start | bytes 580
  10.2 35.5 %copy-start.15 = (f32[96]{0:T(128)S(1)}, f32[96]{0:T(128)}, u32[]{:S(2)}) copy-start(f32[96]{0:T(128)} %constant.105.clone.line_shift_ref) | copy-start | bytes 1156
  10.2 35.5 %copy-start.22 = (f32[96,48]{0,1:T(8,128)S(1)}, f32[96,48]{0,1:T(8,128)}, u32[]{:S(2)}) copy-start(f32[96,48]{0,1:T(8,128)} %constant.135) | copy-start | bytes 55300
  10.2 35.5 %copy-start.28 = (f32[96]{0:T(128)S(1)}, f32[96]{0:T(128)}, u32[]{:S(2)}) copy-start(f32[96]{0:T(128)} %constant.113.clone) | copy-start | bytes 1156
  10.2 35.6 %copy-start.21 = (f32[48,96]{1,0:T(8,128)S(1)}, f32[48,96]{1,0:T(8,128)}, u32[]{:S(2)}) copy-start(f32[48,96]{1,0:T(8,128)} %constant.111.clone) | copy-start | bytes 55300
  10.2 35.6 %copy-start.29 = (f32[48]{0:T(128)S(1)}, f32[48]{0:T(128)}, u32[]{:S(2)}) copy-start(f32[48]{0:T(128)} %constant.112.clone) | copy-start | bytes 580
  10.2 35.7 %copy-start.27 = (f32[768]{0:T(1024)S(1)}, f32[768]{0:T(1024)}, u32[]{:S(2)}) copy-start(f32[768]{0:T(1024)} %constant.114.clone) | copy-start | bytes 9220
  10.2 36.6 %copy-start.20 = (f32[7,7,7,1]{0,2,1,3:T(8,128)S(1)}, f32[7,7,7,1]{0,2,1,3:T(8,128)}, u32[]{:S(2)}) copy-start(f32[7,7,7,1]{0,2,1,3:T(8,128)} %constant.136) | copy-start | bytes 4120
  10.3 36.6 %copy-start.26 = (f32[7,7]{1,0:T(8,128)S(1)}, f32[7,7]{1,0:T(8,128)}, u32[]{:S(2)}) copy-start(f32[7,7]{1,0:T(8,128)} %constant.109.clone) | copy-start | bytes 592
  30.1 2.2 %copy-start = (f32[96,48,256]{2,1,0:T(8,128)}, f32[96,48,256]{2,1,0:T(8,128)S(1)}, u32[]{:S(2)}) copy-start(f32[96,48,256]{2,1,0:T(8,128)S(1)} %get-tuple-element.8.spectrum_ref) | copy-start | bytes 14155780
  32.3 26.4 %copy-start.18 = (f32[768,768,1]{1,0,2:T(8,128)S(1)}, f32[768,768,1]{1,0,2:T(8,128)}, u32[]{:S(2)}) copy-start(f32[768,768,1]{1,0,2:T(8,128)} %constant.137) | copy-start | bytes 7077892
  32.8 28.4 %copy-start.24 = (f32[15,15,1]{1,0,2:T(8,128)S(1)}, f32[15,15,1]{1,0,2:T(8,128)}, u32[]{:S(2)}) copy-start(f32[15,15,1]{1,0,2:T(8,128)} %constant.138) | copy-start | bytes 2704
  32.8 28.4 %copy-start.34 = (f32[15]{0:T(128)S(1)}, f32[15]{0:T(128)}, u32[]{:S(2)}) copy-start(f32[15]{0:T(128)} %constant.116.clone) | copy-start | bytes 184
  34.0 23.7 %all-to-all-start = ((f32[128,2,288]{2,1,0:T(2,128)}), f32[128,2,288]{2,1,0:T(2,128)S(1)}, u32[]{:S(2)}, u32[]{:S(2)}) async-start(f32[128,2,288]{2,1,0:T(2,128)} %reshape.225), calls=%async_computation | async-start | bytes 786432 | tf_op jit(solution)/shard_map/all_to_all | solution.py:452
  58.6 5.8 %copy-start.33 = (f32[8,7]{1,0:T(8,128)S(1)}, f32[8,7]{1,0:T(8,128)}, u32[]{:S(2)}) copy-start(f32[8,7]{1,0:T(8,128)} %constant.119.clone) | copy-start | bytes 676
  58.6 6.0 %copy-start.32 = (f32[7,8]{1,0:T(8,128)S(1)}, f32[7,8]{1,0:T(8,128)}, u32[]{:S(2)}) copy-start(f32[7,8]{1,0:T(8,128)} %constant.120.clone) | copy-start | bytes 676
  58.7 6.2 %copy-start.25 = (f32[16,15]{1,0:T(8,128)S(1)}, f32[16,15]{1,0:T(8,128)}, u32[]{:S(2)}) copy-start(f32[16,15]{1,0:T(8,128)} %constant.122.clone) | copy-start | bytes 2884
  58.8 6.3 %copy-start.31 = (f32[7,8]{1,0:T(8,128)S(1)}, f32[7,8]{1,0:T(8,128)}, u32[]{:S(2)}) copy-start(f32[7,8]{1,0:T(8,128)} %constant.121.clone) | copy-start | bytes 676
  63.2 19.6 %copy-start.3 = (f32[2,48,256]{2,1,0:T(8,128)S(1)}, f32[2,48,256]{2,1,0:T(8,128)}, u32[]{:S(2)}) copy-start(f32[2,48,256]{2,1,0:T(8,128)} %constant.104.clone.faces_ref) | copy-start | bytes 294916
  63.3 19.6 %copy-start.5 = (f32[48,256]{1,0:T(8,128)S(1)}, f32[48,256]{1,0:T(8,128)}, u32[]{:S(2)}) copy-start(f32[48,256]{1,0:T(8,128)} %constant.103.clone.shift_ref) | copy-start | bytes 147460
  63.3 19.6 %copy-start.6 = (bf16[256,256]{1,0:T(8,128)(2,1)S(1)}, bf16[256,256]{1,0:T(8,128)(2,1)}, u32[]{:S(2)}) copy-start(bf16[256,256]{1,0:T(8,128)(2,1)} %constant.124.clone.depth_low_ref) | copy-start | bytes 393220
  63.3 19.6 %copy-start.7 = (bf16[256,256]{1,0:T(8,128)(2,1)S(1)}, bf16[256,256]{1,0:T(8,128)(2,1)}, u32[]{:S(2)}) copy-start(bf16[256,256]{1,0:T(8,128)(2,1)} %constant.123.clone.depth_high_ref) | copy-start | bytes 393220
  63.3 19.6 %copy-start.10 = (bf16[192,192]{1,0:T(8,128)(2,1)S(1)}, bf16[192,192]{1,0:T(8,128)(2,1)}, u32[]{:S(2)}) copy-start(bf16[192,192]{1,0:T(8,128)(2,1)} %constant.125.clone.line_ref) | copy-start | bytes 221188
  63.3 19.6 %copy-start.12 = (bf16[96,96]{1,0:T(8,128)(2,1)S(1)}, bf16[96,96]{1,0:T(8,128)(2,1)}, u32[]{:S(2)}) copy-start(bf16[96,96]{1,0:T(8,128)(2,1)} %constant.126.clone.row_ref) | copy-start | bytes 55300
  63.3 19.6 %copy-start.17 = (f32[96]{0:T(128)S(1)}, f32[96]{0:T(128)}, u32[]{:S(2)}) copy-start(f32[96]{0:T(128)} %constant.106.clone.line_face_ref) | copy-start | bytes 1156
  82.9 2.3 %copy-start.1 = (f32[96,48,256]{2,1,0:T(8,128)S(1)}, f32[96,48,256]{2,1,0:T(8,128)}, u32[]{:S(2)}) copy-start(f32[96,48,256]{2,1,0:T(8,128)} %copy-done) | copy-start | bytes 14155780

commit v2 on v1

--- a/solution.py
+++ b/solution.py
@@ -155,6 +155,8 @@
     narrow_ref,
     carry,
     held,
+    wide_face,
+    narrow_face,
 ):
     step = pl.program_id(0)
     rows, lines = row_ref.shape[0] // 2, line_ref.shape[0] // 2
@@ -164,7 +166,6 @@
     @pl.when(step == 0)
     def _():
         carry[...] = jnp.zeros_like(carry)
-        narrow_ref[...] = jnp.zeros_like(narrow_ref)
 
     @pl.when(step < steps)
     def _():
@@ -177,11 +178,20 @@
             part = below - here + lower_neighbour(second_ref[i], 0) + lower_neighbour(third_ref[i], 1)
             below = here
             parts.append(part)
+            narrow_face[pl.ds(step * block + i, 1), :] = second_ref[i, lines - 1 : lines, :]
         carry[...] = below
         stacked = from_right(jnp.concatenate(parts, axis=0), depth_high_ref[...], depth_low_ref[...])
         for i in range(block):
             part = from_left(line_ref[...], stacked[i * lines : (i + 1) * lines])
             put(held, pl.ds(pl.multiple_of((step * block + i) * lines, 8), lines), part)
+
+    @pl.when(step == steps)
+    def _():
+        face = from_right(first_ref[block - 1], depth_high_ref[...], depth_low_ref[...])
+        wide_face[...] = from_left(line_ref[...], face)
+        face = from_right(narrow_face[...], depth_high_ref[...], depth_low_ref[...])
+        narrow_ref[0] = jnp.zeros_like(face)
+        narrow_ref[1] = from_left(row_ref[...], face)
 
     @pl.when(step >= steps)
     def _():
@@ -192,15 +202,15 @@
             part = from_left(row_ref[...], take(held, pl.ds(line, rows, stride=lines)))
             out_ref[i] = part
             eig = shift_ref[...] + line_shift_ref[line]
-            good = eig > 0.0
-            closed = jnp.where(good, part / jnp.where(good, eig, 1.0), 0.0)
+            closed = jnp.where(eig > 0.0, part / eig, 0.0)
             lows.append(jnp.sum(closed * faces_ref[0], axis=0, keepdims=True))
             highs.append(jnp.sum(closed * faces_ref[1], axis=0, keepdims=True))
             closed = closed * line_face_ref[line]
             narrow_low = narrow_low + closed
             narrow_high = narrow_high + closed if i % 2 == 0 else narrow_high - closed
         wide_ref[0] = jnp.concatenate(lows, axis=0)
-        wide_ref[1] = jnp.concatenate(highs, axis=0)
+        here = pl.ds(pl.multiple_of((step - steps) * group, 8), group)
+        wide_ref[1] = jnp.concatenate(highs, axis=0) + wide_face[here, :]
         narrow_ref[0] = narrow_low
         narrow_ref[1] = narrow_high
 
@@ -235,8 +245,7 @@
             turned = narrow_ref[1] if i % 2 == 0 else -narrow_ref[1]
             part = spectrum_ref[i] + added + line_face_ref[line] * (turned - narrow_ref[0])
             eig = shift_ref[...] + line_shift_ref[line]
-            good = eig > 0.0
-            part = jnp.where(good, part / jnp.where(good, eig, 1.0), level_ref[...])
+            part = jnp.where(eig > 0.0, part / eig, level_ref[...])
             put(held, pl.ds(line, rows, stride=lines), from_left(row_ref[...], part))
 
     @pl.when(step >= steps)
@@ -250,8 +259,9 @@
             out_ref[i] = result[i * lines : (i + 1) * lines]
 
 
-BLOCK = 4
-GROUP = 8
+VMEM_LIMIT = 60 * 2**20
+BLOCK = 16
+GROUP = 16
 
 
 def box_tables(rows, lines, depth):
@@ -299,8 +309,13 @@
             pl.BlockSpec((2, GROUP, depth), lambda s: (0, jnp.maximum(s - steps, 0), 0)),
             whole(2, rows, depth),
         ],
-        scratch_shapes=[pltpu.VMEM((lines, depth), f32), pltpu.VMEM((depth // LANES, rows * lines, LANES), f32)],
-        compiler_params=pltpu.CompilerParams(vmem_limit_bytes=48 * 2**20),
+        scratch_shapes=[
+            pltpu.VMEM((lines, depth), f32),
+            pltpu.VMEM((depth // LANES, rows * lines, LANES), f32),
+            pltpu.VMEM((lines, depth), f32),
+            pltpu.VMEM((rows, depth), f32),
+        ],
+        compiler_params=pltpu.CompilerParams(vmem_limit_bytes=VMEM_LIMIT),
     )(
         first,
         second,
@@ -330,7 +345,7 @@
         + table_specs(rows, lines, depth),
         out_specs=pl.BlockSpec((BLOCK, lines, depth), lambda s: (jnp.maximum(s - groups, 0), 0, 0)),
         scratch_shapes=[pltpu.VMEM((depth // LANES, rows * lines, LANES), jnp.float32)],
-        compiler_params=pltpu.CompilerParams(vmem_limit_bytes=48 * 2**20),
+        compiler_params=pltpu.CompilerParams(vmem_limit_bytes=VMEM_LIMIT),
     )(
         spectrum,
         wide_flux,
@@ -437,17 +452,8 @@
     place = wide_place * narrow + narrow_place
     devices = wide * narrow
     t = tables(rows, lines, depth, wide, narrow)
-    row_table = jnp.asarray(cosine_matrix(rows), jnp.float32)
-    line_table = jnp.asarray(cosine_matrix(lines), jnp.float32)
-    depth_table = jnp.asarray(cosine_matrix(depth), jnp.float32)
     spectrum, wide_traces, narrow_traces = forward(slope_first, slope_second, slope_third)
-    slope_wide = jnp.einsum("yz,rz->yr", slope_first[-1], depth_table, precision=HIGHEST)
-    slope_wide = jnp.einsum("yr,ky->kr", slope_wide, line_table, precision=HIGHEST)
-    slope_narrow = jnp.einsum("xz,rz->xr", slope_second[:, -1], depth_table, precision=HIGHEST)
-    slope_narrow = jnp.einsum("xr,kx->kr", slope_narrow, row_table, precision=HIGHEST)
-    traces = jnp.concatenate(
-        [wide_traces[0], wide_traces[1] + slope_wide, narrow_traces[0], narrow_traces[1] + slope_narrow], axis=0
-    )
+    traces = jnp.concatenate([wide_traces.reshape(2 * lines, depth), narrow_traces.reshape(2 * rows, depth)], axis=0)
     traces = jnp.transpose(traces).reshape(devices, depth // devices, -1)
     traces = lax.all_to_all(traces, ("wide", "narrow"), split_axis=0, concat_axis=0, tiled=True)
     fluxes = interfaces(traces, t, place, rows, lines, depth, wide, narrow)

time: 102 us -> 83.8 us (0.82)
  local copies, waits for them, and re-layouts: 15.1 us -> 6.88 us
  Pallas kernels: 36 us -> 29.4 us
  matrix products: 9.71 us -> 6.64 us
    unnamed x70 -> x32, local copies, waits for them, and re-layouts: 11.1 us -> 0.11 us
    pallas_call x1, Pallas kernels: 19.8 us -> 16.4 us  [forward(): pl.pallas_call(functools.partial(forward_kernel, steps), grid=(steps + gr...]
    pallas_call x1, Pallas kernels: 16.2 us -> 13 us  [inverse(): pl.pallas_call(functools.partial(inverse_kernel, groups), grid=(steps + g...]
    dot_general x4 -> x0, matrix products: 3.07 us -> none  [the longest x1 1.36 us: shards(): jnp.einsum('yz,rz->yr', slope_first[-1], depth_table, precision=HIGHEST)]
    reshape x0 -> x2, local copies, waits for them, and re-layouts: none -> 2.07 us  [the longest x1 1.09 us: shards(): wide_traces.reshape(2 * lines, depth)]
    slice x1 -> x0, local copies, waits for them, and re-layouts: 1.04 us -> none  [shards(): slope_second[:, -1]]
  transfers between devices with their start and end apart: 1 -> 1, of which waited for: 1 -> 1; matrix products, arithmetic and copies ran while one was open for 2% -> 3% of each run, Pallas kernels for 0% -> 0%
where the time goes in v2:
time: 83.8 us; the launch traced here: 83.4 us
  Pallas kernels  29.4 us (35%)
  blocking collectives  16.4 us (20%)
  starting transfers between devices  11.5 us (14%)
  waiting for transfers between devices  10 us (12%)
  local copies, waits for them, and re-layouts  6.88 us (8%)
  matrix products  6.64 us (8%)
  other arithmetic  2.16 us (3%)
    pallas_call x1, Pallas kernels, forward(): pl.pallas_call(functools.partial(forward_kernel, steps), grid=(steps + gr...  16.4 us
    all_to_all x1, blocking collectives, shards(): lax.all_to_all(fluxes, ('wide', 'narrow'), split_axis=0, concat_axis=0, t...  16.4 us
    pallas_call x1, Pallas kernels, inverse(): pl.pallas_call(functools.partial(inverse_kernel, groups), grid=(steps + g...  13 us
    all_to_all x1, starting transfers between devices, shards(): lax.all_to_all(traces, ('wide', 'narrow'), split_axis=0, concat_axis=0, t...  11.5 us
    all_to_all x1, waiting for transfers between devices, shards(): lax.all_to_all(traces, ('wide', 'narrow'), split_axis=0, concat_axis=0, t...  10 us
    dot_general x1, matrix products, interfaces(): joined = jnp.einsum('riy,qy->riq', jump_wide, t['join'], precision=HIGHEST)  2.24 us
  transfers between devices with their start and end apart: 1, of which 1 were waited for; matrix products, arithmetic and copies ran while one was open for 3% of the time, Pallas kernels for 0%

profile of v2, /device:TPU:1, one launch (start us, length us, event | category | flops | bytes accessed | tf_op | source)
XLA Modules:
  0.0 83.4 jit_solution(15728395045726261163)
XLA Ops:
  0.0 16.4 %shard_map.370 = (f32[96,48,256]{2,1,0:T(8,128)}, f32[2,96,256]{2,1,0:T(8,128)}, f32[2,48,256]{2,1,0:T(8,128)}) custom-call(f32[48,96,256]{2,1,0:T(8,128)} %first_ref.1, f32[48,96,256]{2,1,0:T(8,128)} %second_ref.1, f32[48,96,256]{2,1,0:T(8,128)} %third_ref.1, bf16[256,256]{1,0:T(8,128)(2,1)} %constant.38.clone.depth_high_ref, ...), custom_call_target="tpu_custom_call" | custom-call | tf_op jit(solution)/shard_map/pallas_call | solution.py:298
  16.4 0.0 copy-start.3
  16.4 0.0 copy-start.4
  16.5 1.1 %copy.77 = f32[192,256]{0,1:T(8,128)S(1)} copy(f32[192,256]{1,0:T(8,128)} %bitcast.111) | data formatting | bytes 393216 | tf_op jit(solution)/shard_map/reshape | solution.py:456
  17.6 1.0 %copy.78 = f32[96,256]{0,1:T(8,128)S(1)} copy(f32[96,256]{1,0:T(8,128)} %bitcast.112) | data formatting | bytes 196608 | tf_op jit(solution)/shard_map/reshape | solution.py:456
  18.6 0.1 maximum_bitcast_fusion
  18.8 1.0 %reshape.233 = f32[128,2,288]{2,1,0:T(2,128)} reshape(f32[256,288]{1,0:T(8,128)S(1)} %maximum_bitcast_fusion) | data formatting | bytes 589824 | tf_op jit(solution)/shard_map/reshape | solution.py:457
  19.7 11.5 %all-to-all-start = ((f32[128,2,288]{2,1,0:T(2,128)}), f32[128,2,288]{2,1,0:T(2,128)S(1)}, u32[]{:S(2)}, u32[]{:S(2)}) async-start(f32[128,2,288]{2,1,0:T(2,128)} %reshape.233), calls=%async_computation | async-start | bytes 786432 | tf_op jit(solution)/shard_map/all_to_all | solution.py:458
  31.3 0.1 broadcast_and_fusion
  31.4 0.1 broadcast_add_fusion
  31.5 0.1 and_select_fusion
  31.6 0.1 divide_select_fusion
  31.7 0.8 fusion.17
  32.6 0.9 %broadcast_select_fusion.1 = (f32[2,7,7,48]{3,2,1,0:T(8,128)S(1)}, f32[2,7,7,48]{3,2,1,0:T(8,128)S(1)}) fusion(f32[7,7]{1,0:T(8,128)S(1)} %copy-done.7, pred[2,48]{1,0:T(4,128)(4,1)S(1)} %broadcast_and_fusion, f32[7,7,7,1]{0,2,1,3:T(8,128)S(1)} %copy-done.1, f32[256,7,48]{2,1,0:T(8,128)} %constant.98.clone, s32[]{:T(128)S(6)} %select_n.72), kind=kOutput, calls=%fused_computation.48 | convolution fusion | flops 399840 | bytes 47492 | tf_op jit(solution)/shard_map/mjl,rmk->rjlk/dot_general | solution.py:388
  33.5 10.0 %all-to-all-done = f32[128,2,288]{2,1,0:T(2,128)S(1)} async-done(((f32[128,2,288]{2,1,0:T(2,128)}), f32[128,2,288]{2,1,0:T(2,128)S(1)}, u32[]{:S(2)}, u32[]{:S(2)}) %all-to-all-start) | async-done | bytes 294944 | tf_op jit(solution)/shard_map/all_to_all | solution.py:458
  43.5 0.1 copy.109
  43.6 0.1 slice_subtract_fusion.2
  43.7 0.1 multiply_reduce_fusion.1
  43.9 0.3 convolution_bitcast_fusion.1
  44.2 0.1 fusion.2
  44.4 0.1 reshape.252
  44.5 2.2 %fusion.25 = f32[2,15,768]{2,1,0:T(8,128)S(1)} fusion(f32[2,15,768]{2,1,0:T(8,128)S(1)} %reshape.252, f32[768,768,1]{1,0,2:T(8,128)S(1)} %copy-done), kind=kOutput, calls=%fused_computation.75 | convolution fusion | flops 212336640 | bytes 2543616 | tf_op jit(solution)/shard_map/riy,qy->riq/dot_general | solution.py:418
  46.8 0.1 slice_reduce_fusion.1
  46.9 0.2 fusion
  47.1 0.3 convolution_bitcast_fusion.2
  47.4 1.5 %fusion.26 = f32[2,15,768]{2,1,0:T(8,128)S(1)} fusion(f32[2,15,768]{2,1,0:T(8,128)S(1)} %convolution_bitcast_fusion.2, f32[768,768,1]{1,0,2:T(8,128)S(1)} %copy-done), kind=kOutput, calls=%fused_computation.76 | convolution fusion | flops 212336640 | bytes 2543616 | tf_op jit(solution)/shard_map/riq,qy->riy/dot_general | solution.py:422
  48.9 0.1 reshape.253
  49.1 0.1 fusion.11
  49.2 0.5 convolution_bitcast_fusion
  49.8 0.1 fusion.4
  49.9 0.1 slice_reduce_fusion
  50.0 0.1 multiply_reduce_fusion
  50.1 0.2 fusion.27
  50.3 0.2 fusion.28
  50.5 0.1 broadcast_select_fusion
  50.6 0.1 convolution_bitcast_fusion.5
  50.7 0.2 fusion.1
  50.9 0.1 broadcast_in_dim.81
  51.0 0.2 concatenate.7
  51.3 0.1 copy.110
  51.4 0.3 copy.89
  51.7 16.4 %all_to_all.10 = f32[128,2,296]{2,1,0:T(2,128)S(1)} all-to-all(f32[128,2,296]{2,1,0:T(2,128)S(1)} %copy.89), channel_id=1, replica_groups=mesh['wide'=16,'narrow'=8] {'wide','narrow'}, dimensions={0} | all-to-all | bytes 606208 | tf_op jit(solution)/shard_map/all_to_all | solution.py:460
  68.1 0.3 reshape.238
  68.4 0.1 copy.90
  68.5 0.6 slice.104.level_ref
  69.1 0.6 slice.103
  69.7 0.7 slice.102
  70.4 13.0 %shard_map.371 = f32[48,96,256]{2,1,0:T(8,128)} custom-call(f32[96,48,256]{2,1,0:T(8,128)} %get-tuple-element.8.spectrum_ref, f32[2,96,256]{2,1,0:T(8,128)} %bitcast.109, f32[2,48,256]{2,1,0:T(8,128)} %bitcast.110, f32[1,256]{1,0:T(1,128)} %slice.104.level_ref, bf16[256,256]{1,0:T(8,128)(2,1)} %constant.114.clone.depth_high_ref, ...), custom_call_target="tpu_custom_call" | custom-call | tf_op jit(solution)/shard_map/pallas_call | solution.py:335
  (40 shorter events, 0.3 us)
Async XLA Ops:
  16.4 15.0 %copy-start.11 = (f32[48]{0:T(128)S(1)}, f32[48]{0:T(128)}, u32[]{:S(2)}) copy-start(f32[48]{0:T(128)} %constant.101.clone) | copy-start | bytes 580
  16.4 15.0 %copy-start.3 = (f32[96,48]{0,1:T(8,128)S(1)}, f32[96,48]{0,1:T(8,128)}, u32[]{:S(2)}) copy-start(f32[96,48]{0,1:T(8,128)} %constant.126) | copy-start | bytes 55300
  16.4 15.0 %copy-start.4 = (f32[96]{0:T(128)S(1)}, f32[96]{0:T(128)}, u32[]{:S(2)}) copy-start(f32[96]{0:T(128)} %constant.96.clone.line_shift_ref) | copy-start | bytes 1156
  16.5 15.0 %copy-start.9 = (f32[96]{0:T(128)S(1)}, f32[96]{0:T(128)}, u32[]{:S(2)}) copy-start(f32[96]{0:T(128)} %constant.104.clone) | copy-start | bytes 1156
  16.5 15.1 %copy-start.2 = (f32[48,96]{1,0:T(8,128)S(1)}, f32[48,96]{1,0:T(8,128)}, u32[]{:S(2)}) copy-start(f32[48,96]{1,0:T(8,128)} %constant.102.clone) | copy-start | bytes 55300
  16.5 15.1 %copy-start.10 = (f32[48]{0:T(128)S(1)}, f32[48]{0:T(128)}, u32[]{:S(2)}) copy-start(f32[48]{0:T(128)} %constant.103.clone) | copy-start | bytes 580
  16.5 15.2 %copy-start.8 = (f32[768]{0:T(1024)S(1)}, f32[768]{0:T(1024)}, u32[]{:S(2)}) copy-start(f32[768]{0:T(1024)} %constant.105.clone) | copy-start | bytes 9220
  16.5 16.1 %copy-start.1 = (f32[7,7,7,1]{0,2,1,3:T(8,128)S(1)}, f32[7,7,7,1]{0,2,1,3:T(8,128)}, u32[]{:S(2)}) copy-start(f32[7,7,7,1]{0,2,1,3:T(8,128)} %constant.127) | copy-start | bytes 4120
  16.5 16.1 %copy-start.7 = (f32[7,7]{1,0:T(8,128)S(1)}, f32[7,7]{1,0:T(8,128)}, u32[]{:S(2)}) copy-start(f32[7,7]{1,0:T(8,128)} %constant.100.clone) | copy-start | bytes 592
  19.7 24.8 %copy-start = (f32[768,768,1]{1,0,2:T(8,128)S(1)}, f32[768,768,1]{1,0,2:T(8,128)}, u32[]{:S(2)}) copy-start(f32[768,768,1]{1,0,2:T(8,128)} %constant.128) | copy-start | bytes 7077892
  19.7 23.7 %all-to-all-start = ((f32[128,2,288]{2,1,0:T(2,128)}), f32[128,2,288]{2,1,0:T(2,128)S(1)}, u32[]{:S(2)}, u32[]{:S(2)}) async-start(f32[128,2,288]{2,1,0:T(2,128)} %reshape.233), calls=%async_computation | async-start | bytes 786432 | tf_op jit(solution)/shard_map/all_to_all | solution.py:458
  43.8 3.0 %copy-start.5 = (f32[15,15,1]{1,0,2:T(8,128)S(1)}, f32[15,15,1]{1,0,2:T(8,128)}, u32[]{:S(2)}) copy-start(f32[15,15,1]{1,0,2:T(8,128)} %constant.129) | copy-start | bytes 2704
  43.8 3.0 %copy-start.15 = (f32[15]{0:T(128)S(1)}, f32[15]{0:T(128)}, u32[]{:S(2)}) copy-start(f32[15]{0:T(128)} %constant.107.clone) | copy-start | bytes 184
  47.4 2.7 %copy-start.14 = (f32[8,7]{1,0:T(8,128)S(1)}, f32[8,7]{1,0:T(8,128)}, u32[]{:S(2)}) copy-start(f32[8,7]{1,0:T(8,128)} %constant.110.clone) | copy-start | bytes 676
  47.4 2.8 %copy-start.13 = (f32[7,8]{1,0:T(8,128)S(1)}, f32[7,8]{1,0:T(8,128)}, u32[]{:S(2)}) copy-start(f32[7,8]{1,0:T(8,128)} %constant.111.clone) | copy-start | bytes 676
  48.9 1.7 %copy-start.6 = (f32[16,15]{1,0:T(8,128)S(1)}, f32[16,15]{1,0:T(8,128)}, u32[]{:S(2)}) copy-start(f32[16,15]{1,0:T(8,128)} %constant.113.clone) | copy-start | bytes 2884
  48.9 1.8 %copy-start.12 = (f32[7,8]{1,0:T(8,128)S(1)}, f32[7,8]{1,0:T(8,128)}, u32[]{:S(2)}) copy-start(f32[7,8]{1,0:T(8,128)} %constant.112.clone) | copy-start | bytes 676

commit v3 on v2

--- a/solution.py
+++ b/solution.py
@@ -245,7 +245,7 @@
             turned = narrow_ref[1] if i % 2 == 0 else -narrow_ref[1]
             part = spectrum_ref[i] + added + line_face_ref[line] * (turned - narrow_ref[0])
             eig = shift_ref[...] + line_shift_ref[line]
-            part = jnp.where(eig > 0.0, part / eig, level_ref[...])
+            part = jnp.where(eig > 0.0, part / eig, level_ref[:1])
             put(held, pl.ds(line, rows, stride=lines), from_left(row_ref[...], part))
 
     @pl.when(step >= steps)
@@ -257,6 +257,132 @@
         result = from_right(jnp.concatenate(parts, axis=0), depth_high_ref[...], depth_low_ref[...])
         for i in range(block):
             out_ref[i] = result[i * lines : (i + 1) * lines]
+
+
+MESH = pl.DeviceIdType.MESH
+
+
+def greet(wide, narrow):
+    w, n = lax.axis_index("wide"), lax.axis_index("narrow")
+    barrier = pltpu.get_barrier_semaphore()
+    for d in range(1, narrow):
+        pl.semaphore_signal(barrier, inc=1, device_id=(w, lax.rem(n + d, narrow)), device_id_type=MESH)
+    for d in range(1, wide):
+        pl.semaphore_signal(barrier, inc=1, device_id=(lax.rem(w + d, wide), n), device_id_type=MESH)
+    pl.semaphore_wait(barrier, wide + narrow - 2)
+
+
+def trade(axis, source, target, send, recv):
+    w, n = lax.axis_index("wide"), lax.axis_index("narrow")
+    peers = source.shape[0]
+    here = w if axis == "wide" else n
+    copies = []
+    for d in range(1, peers):
+        to = lax.rem(here + d, peers)
+        copies.append(
+            pltpu.make_async_remote_copy(
+                src_ref=source.at[to],
+                dst_ref=target.at[here],
+                send_sem=send.at[d],
+                recv_sem=recv.at[d],
+                device_id=(to, n) if axis == "wide" else (w, to),
+                device_id_type=MESH,
+            )
+        )
+    for copy in copies:
+        copy.start()
+    target[here] = source[here]
+    for copy in copies:
+        copy.wait()
+
+
+def turn(source, target):
+    outer = source.shape[0]
+    inner = target.shape[0]
+    count = source.shape[1] // inner
+    for a in range(outer):
+        for b in range(inner):
+            target[b, a * count : (a + 1) * count, :] = source[a, b * count : (b + 1) * count, :]
+
+
+def gather_kernel(wide_ref, narrow_ref, out_ref, first, near, turned, near_send, near_recv, far_send, far_recv):
+    narrow, far_rows, width = first.shape
+    wide = turned.shape[0]
+    parts = [wide_ref[0], wide_ref[1], narrow_ref[0], narrow_ref[1]]
+    depth = parts[0].shape[1]
+    parts.append(jnp.zeros((width - sum(p.shape[0] for p in parts), depth), jnp.float32))
+    values = jnp.concatenate(parts, axis=0).T
+    for p in range(narrow):
+        first[p] = values[p * far_rows : (p + 1) * far_rows]
+    greet(wide, narrow)
+    trade("narrow", first, near, near_send, near_recv)
+    turn(near, turned)
+    trade("wide", turned, out_ref, far_send, far_recv)
+
+
+def scatter_kernel(in_ref, wide_ref, narrow_ref, level_ref, far, turned, near, near_send, near_recv, far_send, far_recv):
+    narrow = near.shape[0]
+    wide = far.shape[0]
+    greet(wide, narrow)
+    trade("wide", in_ref, far, far_send, far_recv)
+    turn(far, turned)
+    trade("narrow", turned, near, near_send, near_recv)
+    values = jnp.concatenate([near[p] for p in range(narrow)], axis=0).T
+    lines, rows = wide_ref.shape[1], narrow_ref.shape[1]
+    wide_ref[0] = values[:lines]
+    wide_ref[1] = values[lines : 2 * lines]
+    narrow_ref[0] = values[2 * lines : 2 * lines + rows]
+    narrow_ref[1] = values[2 * lines + rows : 2 * (lines + rows)]
+    level_ref[...] = values[2 * (lines + rows) : 2 * (lines + rows) + 8]
+
+
+def message_width(rows, lines):
+    return -(-(2 * (rows + lines) + 8) // LANES) * LANES
+
+
+IN_VMEM = pl.BlockSpec(memory_space=pltpu.VMEM)
+
+
+def semaphores(wide, narrow):
+    return [pltpu.SemaphoreType.DMA((k,)) for k in (narrow, narrow, wide, wide)]
+
+
+def gather(wide_traces, narrow_traces, wide, narrow):
+    lines, depth = wide_traces.shape[1:]
+    rows = narrow_traces.shape[1]
+    count = depth // (wide * narrow)
+    width = message_width(rows, lines)
+    near = (narrow, wide * count, width)
+    far = (wide, narrow * count, width)
+    return pl.pallas_call(
+        gather_kernel,
+        out_shape=jax.ShapeDtypeStruct(far, jnp.float32),
+        in_specs=[IN_VMEM, IN_VMEM],
+        out_specs=IN_VMEM,
+        scratch_shapes=[pltpu.VMEM(v, jnp.float32) for v in (near, near, far)] + semaphores(wide, narrow),
+        compiler_params=pltpu.CompilerParams(collective_id=0, has_side_effects=True),
+    )(wide_traces, narrow_traces)
+
+
+def scatter(fluxes, rows, lines, depth):
+    wide, _, width = fluxes.shape
+    narrow = lax.axis_size("narrow")
+    count = depth // (wide * narrow)
+    near = (narrow, wide * count, width)
+    far = (wide, narrow * count, width)
+    f32 = jnp.float32
+    return pl.pallas_call(
+        scatter_kernel,
+        out_shape=[
+            jax.ShapeDtypeStruct((2, lines, depth), f32),
+            jax.ShapeDtypeStruct((2, rows, depth), f32),
+            jax.ShapeDtypeStruct((8, depth), f32),
+        ],
+        in_specs=[IN_VMEM],
+        out_specs=[IN_VMEM] * 3,
+        scratch_shapes=[pltpu.VMEM(v, f32) for v in (far, near, near)] + semaphores(wide, narrow),
+        compiler_params=pltpu.CompilerParams(collective_id=1, has_side_effects=True),
+    )(fluxes)
 
 
 VMEM_LIMIT = 60 * 2**20
@@ -340,7 +466,7 @@
             pl.BlockSpec((GROUP, rows, depth), lambda s: (jnp.minimum(s, groups - 1), 0, 0)),
             pl.BlockSpec((2, GROUP, depth), lambda s: (0, jnp.minimum(s, groups - 1), 0)),
             whole(2, rows, depth),
-            whole(1, depth),
+            whole(8, depth),
         ]
         + table_specs(rows, lines, depth),
         out_specs=pl.BlockSpec((BLOCK, lines, depth), lambda s: (jnp.maximum(s - groups, 0), 0, 0)),
@@ -373,11 +499,11 @@
 
 
 def interfaces(traces, t, place, rows, lines, depth, wide, narrow):
-    count = traces.shape[1]
+    count = traces.shape[1] // narrow
     traces = traces.reshape(wide, narrow, count, -1)
     traces = jnp.transpose(traces, (2, 0, 1, 3))
-    cut = [lines, 2 * lines, 2 * lines + rows]
-    wide_low, wide_high, narrow_low, narrow_high = jnp.split(traces, cut, axis=-1)
+    cut = [lines, 2 * lines, 2 * lines + rows, 2 * (lines + rows)]
+    wide_low, wide_high, narrow_low, narrow_high, _ = jnp.split(traces, cut, axis=-1)
     jump_wide = wide_low[:, 1:] - wide_high[:, :-1]
     jump_narrow = narrow_low[:, :, 1:] - narrow_high[:, :, :-1]
     depth_place = place * count + jnp.arange(count)
@@ -435,12 +561,12 @@
         steady[:, None, None, None] & row_zero, balanced[None, :, :, None], flux_narrow
     )
     flux_narrow = jnp.pad(flux_narrow, [(0, 0), (0, 0), (1, 1), (0, 0)])
-    level = jnp.broadcast_to(level[None, :, :, None], (count, wide, narrow, 8))
+    level = jnp.broadcast_to(level[None, :, :, None], (count, wide, narrow, message_width(rows, lines) - 2 * (rows + lines)))
     out = jnp.concatenate(
         [flux_wide[:, :-1], flux_wide[:, 1:], flux_narrow[:, :, :-1], flux_narrow[:, :, 1:], level], axis=-1
     )
     out = jnp.transpose(out, (1, 2, 0, 3))
-    return out.reshape(wide * narrow, count, -1)
+    return out.reshape(wide, narrow * count, -1)
 
 
 def shards(slope_first, slope_second, slope_third):
@@ -449,19 +575,12 @@
     narrow = lax.axis_size("narrow")
     wide_place = lax.axis_index("wide")
     narrow_place = lax.axis_index("narrow")
-    place = wide_place * narrow + narrow_place
-    devices = wide * narrow
+    place = narrow_place * wide + wide_place
     t = tables(rows, lines, depth, wide, narrow)
     spectrum, wide_traces, narrow_traces = forward(slope_first, slope_second, slope_third)
-    traces = jnp.concatenate([wide_traces.reshape(2 * lines, depth), narrow_traces.reshape(2 * rows, depth)], axis=0)
-    traces = jnp.transpose(traces).reshape(devices, depth // devices, -1)
-    traces = lax.all_to_all(traces, ("wide", "narrow"), split_axis=0, concat_axis=0, tiled=True)
+    traces = gather(wide_traces, narrow_traces, wide, narrow)
     fluxes = interfaces(traces, t, place, rows, lines, depth, wide, narrow)
-    fluxes = lax.all_to_all(fluxes, ("wide", "narrow"), split_axis=0, concat_axis=0, tiled=True)
-    fluxes = jnp.transpose(fluxes.reshape(depth, -1))
-    wide_flux = fluxes[: 2 * lines].reshape(2, lines, depth)
-    narrow_flux = fluxes[2 * lines : 2 * (lines + rows)].reshape(2, rows, depth)
-    level = fluxes[2 * (lines + rows) :][:1]
+    wide_flux, narrow_flux, level = scatter(fluxes, rows, lines, depth)
     return inverse(spectrum, wide_flux, narrow_flux, level)
 
 

time: 83.8 us -> 89.2 us (1.064)
  Pallas kernels: 29.4 us -> 73.8 us
  blocking collectives: 16.4 us -> 0 us
  starting transfers between devices: 11.5 us -> 0 us
  waiting for transfers between devices: 10 us -> 0 us
  local copies, waits for them, and re-layouts: 6.88 us -> 3.6 us
  other arithmetic: 2.16 us -> 4.13 us
    pallas_call x0 -> x2, Pallas kernels: none -> 44.4 us  [the longest x1 24.3 us: gather(): pl.pallas_call(gather_kernel, out_shape=jax.ShapeDtypeStruct(far, jnp.flo...]
    all_to_all x1 -> x0, blocking collectives: 16.4 us -> none  [shards(): lax.all_to_all(fluxes, ('wide', 'narrow'), split_axis=0, concat_axis=0, t...]
    all_to_all x1 -> x0, starting transfers between devices: 11.5 us -> none  [shards(): lax.all_to_all(traces, ('wide', 'narrow'), split_axis=0, concat_axis=0, t...]
    all_to_all x1 -> x0, waiting for transfers between devices: 10 us -> none  [shards(): lax.all_to_all(traces, ('wide', 'narrow'), split_axis=0, concat_axis=0, t...]
    reshape x6 -> x1, local copies, waits for them, and re-layouts: 3.76 us -> 1.02 us  [interfaces(): return out.reshape(wide, narrow * count, -1)]
    slice x3 -> x0, local copies, waits for them, and re-layouts: 1.91 us -> none  [the longest x1 0.7 us: shards(): wide_flux = fluxes[:2 * lines].reshape(2, lines, depth)]
    reshape x1 -> x2, local copies, waits for them, and re-layouts: 0.13 us -> 1.35 us  [interfaces(): traces = traces.reshape(wide, narrow, count, -1)]
  transfers between devices with their start and end apart: 1 -> 0, of which waited for: 1 -> 0; matrix products, arithmetic and copies ran while one was open for 3% -> 0% of each run, Pallas kernels for 0% -> 0%
where the time goes in v3:
time: 89.2 us; the launch traced here: 88.6 us
  Pallas kernels  73.8 us (83%)
  matrix products  6.65 us (7%)
  other arithmetic  4.13 us (5%)
  local copies, waits for them, and re-layouts  3.6 us (4%)
    pallas_call x1, Pallas kernels, gather(): pl.pallas_call(gather_kernel, out_shape=jax.ShapeDtypeStruct(far, jnp.flo...  24.3 us
    pallas_call x1, Pallas kernels, scatter(): pl.pallas_call(scatter_kernel, out_shape=[jax.ShapeDtypeStruct((2, lines,...  20 us
    pallas_call x1, Pallas kernels, forward(): pl.pallas_call(functools.partial(forward_kernel, steps), grid=(steps + gr...  16.4 us
    pallas_call x1, Pallas kernels, inverse(): pl.pallas_call(functools.partial(inverse_kernel, groups), grid=(steps + g...  13 us
    dot_general x1, matrix products, interfaces(): joined = jnp.einsum('riy,qy->riq', jump_wide, t['join'], precision=HIGHEST)  2.22 us

profile of v3, /device:TPU:1, one launch (start us, length us, event | category | flops | bytes accessed | tf_op | source)
XLA Modules:
  0.0 88.6 jit_solution(14550373066863579684)
XLA Ops:
  0.1 0.1 broadcast_and_fusion
  0.1 0.7 broadcast_add_fusion
  0.9 0.8 fusion.17
  1.7 0.8 divide_select_fusion
  2.6 0.8 and_select_fusion
  3.4 0.9 %broadcast_select_fusion.1 = (f32[2,7,7,48]{3,2,1,0:T(8,128)S(1)}, f32[2,7,7,48]{3,2,1,0:T(8,128)S(1)}) fusion(f32[7,7]{1,0:T(8,128)} %constant.100.clone, pred[2,48]{1,0:T(4,128)(4,1)S(1)} %broadcast_and_fusion, f32[7,7,7,1]{0,2,1,3:T(8,128)} %constant.127, f32[256,7,48]{2,1,0:T(8,128)} %constant.98.clone, s32[]{:T(128)S(6)} %select_n.72), kind=kOutput, calls=%fused_computation.46 | convolution fusion | flops 399840 | bytes 78692 | tf_op jit(solution)/shard_map/mjl,rmk->rjlk/dot_general | solution.py:514
  4.3 16.4 %shard_map.370 = (f32[96,48,256]{2,1,0:T(8,128)}, f32[2,96,256]{2,1,0:T(8,128)}, f32[2,48,256]{2,1,0:T(8,128)}) custom-call(f32[48,96,256]{2,1,0:T(8,128)} %first_ref.1, f32[48,96,256]{2,1,0:T(8,128)} %second_ref.1, f32[48,96,256]{2,1,0:T(8,128)} %third_ref.1, bf16[256,256]{1,0:T(8,128)(2,1)} %constant.38.clone.depth_high_ref, ...), custom_call_target="tpu_custom_call" | custom-call | tf_op jit(solution)/shard_map/pallas_call | solution.py:424
  20.8 0.0 copy-start.3
  20.8 0.0 copy-start
  20.8 24.3 %shard_map.371 = f32[16,16,384]{2,1,0:T(8,128)} custom-call(f32[2,96,256]{2,1,0:T(8,128)} %get-tuple-element.12.wide_ref, f32[2,48,256]{2,1,0:T(8,128)} %get-tuple-element.13.narrow_ref), custom_call_target="tpu_custom_call" | custom-call | tf_op jit(solution)/shard_map/pallas_call | solution.py:357
  45.2 1.2 %reshape.213 = f32[16,8,2,384]{3,2,1,0:T(2,128)S(1)} reshape(f32[16,16,384]{2,1,0:T(8,128)} %shard_map.371) | data formatting | bytes 786432 | tf_op jit(solution)/shard_map/reshape | solution.py:503
  46.4 0.1 copy.82
  46.5 0.1 slice_subtract_fusion.2
  46.6 0.1 multiply_reduce_fusion.1
  46.7 0.0 copy-start.1
  46.7 0.0 copy-start.8
  46.8 0.3 convolution_bitcast_fusion.1
  47.2 0.1 fusion.2
  47.3 0.1 reshape.228
  47.4 0.0 copy-start.2
  47.4 2.2 %fusion.25 = f32[2,15,768]{2,1,0:T(8,128)S(1)} fusion(f32[2,15,768]{2,1,0:T(8,128)S(1)} %reshape.228, f32[768,768,1]{1,0,2:T(8,128)S(1)} %copy-done), kind=kOutput, calls=%fused_computation.73 | convolution fusion | flops 212336640 | bytes 2543616 | tf_op jit(solution)/shard_map/riy,qy->riq/dot_general | solution.py:544
  49.7 0.0 copy-start.7
  49.7 0.0 copy-start.6
  49.7 0.1 slice_reduce_fusion.1
  49.8 0.0 copy-done.1
  49.8 0.2 fusion
  50.1 0.0 copy-start.4
  50.1 0.3 convolution_bitcast_fusion.2
  50.4 1.4 %fusion.26 = f32[2,15,768]{2,1,0:T(8,128)S(1)} fusion(f32[2,15,768]{2,1,0:T(8,128)S(1)} %convolution_bitcast_fusion.2, f32[768,768,1]{1,0,2:T(8,128)S(1)} %copy-done), kind=kOutput, calls=%fused_computation.74 | convolution fusion | flops 212336640 | bytes 2543616 | tf_op jit(solution)/shard_map/riq,qy->riy/dot_general | solution.py:548
  51.8 0.0 copy-start.5
  51.8 0.1 convolution_bitcast_fusion.5
  51.9 0.1 reshape.229
  52.1 0.1 fusion.11
  52.2 0.2 fusion.27
  52.4 0.2 fusion.28
  52.6 0.5 convolution_bitcast_fusion
  53.1 0.0 copy-done.4
  53.2 0.1 fusion.4
  53.3 0.1 slice_reduce_fusion
  53.4 0.1 multiply_reduce_fusion
  53.5 0.1 broadcast_select_fusion
  53.6 0.2 fusion.1
  53.8 0.1 broadcast_in_dim.81
  53.9 0.2 concatenate.3
  54.2 0.3 copy.66
  54.5 1.0 %reshape.216.in_ref = f32[16,16,384]{2,1,0:T(8,128)} reshape(f32[16,8,2,384]{3,2,1,0:T(2,128)S(1)} %copy.66) | data formatting | bytes 786432 | tf_op jit(solution)/shard_map/reshape | solution.py:569
  55.5 20.0 %shard_map.372 = (f32[2,96,256]{2,1,0:T(8,128)}, f32[2,48,256]{2,1,0:T(8,128)}, f32[8,256]{1,0:T(8,128)}) custom-call(f32[16,16,384]{2,1,0:T(8,128)} %reshape.216.in_ref), custom_call_target="tpu_custom_call" | custom-call | tf_op jit(solution)/shard_map/pallas_call | solution.py:374
  75.6 13.0 %shard_map.373 = f32[48,96,256]{2,1,0:T(8,128)} custom-call(f32[96,48,256]{2,1,0:T(8,128)} %get-tuple-element.11.spectrum_ref, f32[2,96,256]{2,1,0:T(8,128)} %get-tuple-element.14.wide_ref, f32[2,48,256]{2,1,0:T(8,128)} %get-tuple-element.15.narrow_ref, f32[8,256]{1,0:T(8,128)} %get-tuple-element.16.level_ref, ...), custom_call_target="tpu_custom_call" | custom-call | tf_op jit(solution)/shard_map/pallas_call | solution.py:461
  (17 shorter events, 0.3 us)
Async XLA Ops:
  20.8 26.3 %copy-start.3 = (f32[96]{0:T(128)S(1)}, f32[96]{0:T(128)}, u32[]{:S(2)}) copy-start(f32[96]{0:T(128)} %constant.104.clone) | copy-start | bytes 1156
  20.8 26.6 %copy-start = (f32[768,768,1]{1,0,2:T(8,128)S(1)}, f32[768,768,1]{1,0,2:T(8,128)}, u32[]{:S(2)}) copy-start(f32[768,768,1]{1,0,2:T(8,128)} %constant.128) | copy-start | bytes 7077892
  46.7 3.1 %copy-start.1 = (f32[15,15,1]{1,0,2:T(8,128)S(1)}, f32[15,15,1]{1,0,2:T(8,128)}, u32[]{:S(2)}) copy-start(f32[15,15,1]{1,0,2:T(8,128)} %constant.129) | copy-start | bytes 2704
  46.7 3.1 %copy-start.8 = (f32[15]{0:T(128)S(1)}, f32[15]{0:T(128)}, u32[]{:S(2)}) copy-start(f32[15]{0:T(128)} %constant.107.clone) | copy-start | bytes 184
  47.4 4.4 %copy-start.2 = (f32[16,15]{1,0:T(8,128)S(1)}, f32[16,15]{1,0:T(8,128)}, u32[]{:S(2)}) copy-start(f32[16,15]{1,0:T(8,128)} %constant.113.clone) | copy-start | bytes 2884
  49.7 2.5 %copy-start.7 = (f32[8,7]{1,0:T(8,128)S(1)}, f32[8,7]{1,0:T(8,128)}, u32[]{:S(2)}) copy-start(f32[8,7]{1,0:T(8,128)} %constant.110.clone) | copy-start | bytes 676
  49.7 2.7 %copy-start.6 = (f32[7,8]{1,0:T(8,128)S(1)}, f32[7,8]{1,0:T(8,128)}, u32[]{:S(2)}) copy-start(f32[7,8]{1,0:T(8,128)} %constant.111.clone) | copy-start | bytes 676
  50.1 3.1 %copy-start.4 = (f32[48]{0:T(128)S(1)}, f32[48]{0:T(128)}, u32[]{:S(2)}) copy-start(f32[48]{0:T(128)} %constant.103.clone) | copy-start | bytes 580
  51.8 1.8 %copy-start.5 = (f32[7,8]{1,0:T(8,128)S(1)}, f32[7,8]{1,0:T(8,128)}, u32[]{:S(2)}) copy-start(f32[7,8]{1,0:T(8,128)} %constant.112.clone) | copy-start | bytes 676

commit v4 on v3

--- a/solution.py
+++ b/solution.py
@@ -58,36 +58,85 @@
     return (step <= part) - (parts - step) / parts
 
 
+def bordered(matrix, top, left):
+    return np.pad(matrix, ((top, 0), (left, 0)))
+
+
+def lane_padded(table):
+    pad = [(0, 0)] * (table.ndim - 1) + [(0, -table.shape[-1] % LANES)]
+    return np.pad(table, pad)
+
+
 @functools.lru_cache(None)
 def tables(rows, lines, depth, wide, narrow):
-    t = {}
+    count = depth // (wide * narrow)
     row_modes, line_modes, depth_modes = modes(rows), modes(lines), modes(depth)
     row_face, line_face = face(rows), face(lines)
-    sine_n = sine_matrix(narrow)
-    gain = interface_gain(depth_modes[:, None] + row_modes[None, :], lines, narrow)
-    gain[0, 0, :] = 0.0
-    t["narrow_gain"] = np.swapaxes(gain, 1, 2)
-    t["narrow_sines"] = np.einsum("jm,ml->mjl", sine_n, sine_n)
-    levels_n = running_levels(narrow)
-    t["narrow_steady"] = np.cumsum(-levels_n / line_face[0], axis=0)[:-1] / line_face[0]
-    full = cosine_matrix(lines * narrow)
-    local = cosine_matrix(lines)
-    t["join"] = np.einsum("qJn,kn->qJk", full.reshape(lines * narrow, narrow, lines), local).reshape(
-        lines * narrow, lines * narrow
-    )
-    t["wide_decay"] = np.expm1(-exponent(depth_modes[:, None] + modes(lines * narrow)[None, :]) * rows)
-    t["wide_sine"] = sine_matrix(wide)
-    t["wide_angle"] = 1.0 - np.cos(np.pi * np.arange(1, wide) / wide)
-    t["wide_levels"] = -running_levels(wide) / (row_face[0] * math.sqrt(narrow))
+    own_all = np.eye(count)
+    own_first = np.zeros((count, count))
+    own_first[0, 0] = 1.0
+
+    def over_narrow(matrix, own):
+        return np.kron(np.eye(wide), np.kron(matrix, own))
+
+    t = {}
+    t["sine"] = over_narrow(bordered(sine_matrix(narrow), 1, 1), own_all)
+    levels = running_levels(narrow)
+    steady = np.cumsum(-levels / line_face[0], axis=0)[:-1] / line_face[0]
+    t["steady"] = over_narrow(bordered(steady, 1, 1), own_first)
     balance = -(row_face[0] / line_face[0]) * np.tril(np.ones((narrow - 1, narrow)))
-    t["balance"] = balance.T
+    t["balance"] = over_narrow(bordered(balance, 1, 0), own_first)
     k = np.arange(1, lines)
     near = np.sum(line_face[k] ** 2 / line_modes[k])
     far = np.sum(signs(lines)[k] * line_face[k] ** 2 / line_modes[k])
     link = (1.0 + 2.0 * near) * np.eye(narrow - 1) - far * (np.eye(narrow - 1, k=1) + np.eye(narrow - 1, k=-1))
-    t["level_of_flux"] = (levels_n @ link / line_face[0]).T
-    t["level_of_jump"] = (-levels_n / line_face[0]).T
+    t["level_flux"] = over_narrow(bordered(levels @ link / line_face[0], 0, 1), own_first)
+    t["level_jump"] = over_narrow(bordered(-levels / line_face[0], 0, 1), own_first)
+    level_wide = bordered(-running_levels(wide) / (row_face[0] * math.sqrt(narrow)), 0, 1)
+    first_column = np.zeros((count, 1))
+    first_column[0, 0] = 1.0
+    t["level_wide"] = np.kron(first_column.T, np.kron(level_wide, np.kron(np.ones((narrow, 1)), first_column)))
+    gain = interface_gain(depth_modes[:, None] + row_modes[None, :], lines, narrow)
+    gain[0, 0, :] = 0.0
+    gain = bordered(np.moveaxis(gain, 2, 1).reshape(depth * (narrow - 1), rows), 0, 0)
+    gain = np.pad(gain.reshape(depth, narrow - 1, rows), ((0, 0), (1, 0), (0, 0)))
+    gain = gain.reshape(wide * narrow, count, narrow, rows).swapaxes(1, 2)
+    t["gain"] = lane_padded(gain.reshape(wide * narrow, narrow * count, rows))
+    full = cosine_matrix(lines * narrow).reshape(lines * narrow, narrow, lines)
+    t["join"] = np.einsum("qJn,kn->Jkq", full, cosine_matrix(lines))
+    shift = depth_modes[:, None] + modes(lines * narrow)[None, :]
+    decay = np.expm1(-exponent(shift) * rows)
+    top = -np.sqrt(shift / (4.0 + shift)) * decay * (2.0 + decay)
+    t["decay"] = np.stack([decay, top], axis=1).reshape(-1, 8, lines * narrow)
+    t["wide_sine"] = np.kron(own_all, bordered(sine_matrix(wide), 1, 1))
+    angle = 1.0 - np.cos(np.pi * np.arange(wide) / wide)
+    angle[0] = 1.0
+    t["angle"] = np.broadcast_to(angle[:, None], (wide, lines * narrow))
+    t["box_modes"] = row_modes[:, None] + line_modes[None, :]
+    both = row_face[:, None] * line_face[None, :]
+    t["faces"] = np.stack([both, both * signs(rows)[:, None]])
+    t["box_modes_turned"] = t["box_modes"].T
+    t["faces_turned"] = np.stack([both.T, both.T * signs(lines)[:, None]])
+    t["alternate"] = np.broadcast_to(signs(LANES)[None, :], (8, LANES))
     return {name: np.ascontiguousarray(value, dtype=np.float32) for name, value in t.items()}
+
+
+FIXED = (
+    "sine",
+    "steady",
+    "balance",
+    "level_flux",
+    "level_jump",
+    "level_wide",
+    "join",
+    "wide_sine",
+    "angle",
+    "box_modes",
+    "faces",
+    "box_modes_turned",
+    "faces_turned",
+    "alternate",
+)
 
 
 def halves(table):
@@ -305,84 +354,202 @@
             target[b, a * count : (a + 1) * count, :] = source[a, b * count : (b + 1) * count, :]
 
 
-def gather_kernel(wide_ref, narrow_ref, out_ref, first, near, turned, near_send, near_recv, far_send, far_recv):
-    narrow, far_rows, width = first.shape
-    wide = turned.shape[0]
-    parts = [wide_ref[0], wide_ref[1], narrow_ref[0], narrow_ref[1]]
-    depth = parts[0].shape[1]
-    parts.append(jnp.zeros((width - sum(p.shape[0] for p in parts), depth), jnp.float32))
-    values = jnp.concatenate(parts, axis=0).T
+def exact(a, b):
+    return jnp.dot(a, b, precision=HIGHEST, preferred_element_type=jnp.float32)
+
+
+def exact_turned(a, b):
+    return lax.dot_general(
+        a, b, (((1,), (1,)), ((), ())), precision=HIGHEST, preferred_element_type=jnp.float32
+    )
+
+
+def interfaces(traces, t, gain, decay, modes_ref, place, jumps, fluxes, wide, narrow):
+    total = traces.shape[0]
+    count = total // (wide * narrow)
+    span = narrow * count
+    rows, lines = t["box_modes"].shape
+    row = lax.broadcasted_iota(jnp.int32, (total, 1), 0)
+    has_wide = row >= span
+    has_narrow = (row & (span - 1)) >= count
+    own_mode = row & (count - 1)
+    holds_steady = place == 0
+
+    def up(x, by):
+        return pltpu.roll(x, total - by, 0)
+
+    def by_mode(x, weights):
+        out = exact(x, weights[0])
+        for mode in range(1, count):
+            out = jnp.where(own_mode == mode, exact(x, weights[mode]), out)
+        return out
+
+    def influence(box_modes, faces, side, first):
+        weights = []
+        low = lax.broadcasted_iota(jnp.int32, box_modes.shape, 0) == 0
+        left = lax.broadcasted_iota(jnp.int32, box_modes.shape, 1) == 0
+        for mode in range(count):
+            shift = modes_ref[place * count + mode]
+            eig = box_modes[...] + shift
+            some = eig > 0.0
+            value = jnp.where(some, faces[side] / eig, faces[side] if first else 0.0)
+            if first and mode == 0:
+                value = jnp.where(low & jnp.logical_not(left) & holds_steady, 0.0, value)
+            weights.append(value)
+        return weights
+
+    alternate = t["alternate"][:1, :]
+    wide_low, wide_high = traces[:, :lines], traces[:, LANES : LANES + lines]
+    narrow_low, narrow_high = traces[:, 2 * LANES : 2 * LANES + rows], traces[:, 2 * LANES + rows : 2 * LANES + 2 * rows]
+    jump_narrow = jnp.where(has_narrow, narrow_low - pltpu.roll(narrow_high, count, 0), 0.0)
+    jump_wide = jnp.where(has_wide, wide_low - pltpu.roll(wide_high, span, 0), 0.0)
+    gain = jnp.concatenate([gain[:, :rows]] * wide, axis=0)
+    sine = t["sine"][...]
+
+    def glued(jump):
+        return exact(sine, gain * exact(sine, jump))
+
+    row_zero = lax.broadcasted_iota(jnp.int32, (total, rows), 1) == 0
+    flux = glued(jump_narrow)
+    steady = exact(t["steady"][...], jump_narrow)
+    flux = flux + jnp.where(row_zero & holds_steady, steady, 0.0)
+    moved = []
+    for side in range(2):
+        value = by_mode(flux, influence(t["box_modes"], t["faces"], side, True))
+        moved.append(alternate[:, :lines] * up(value, count) - value)
+    jump_wide = jump_wide + jnp.where(has_wide, moved[0] - pltpu.roll(moved[1], span, 0), 0.0)
+    pad = jnp.zeros((total, LANES - lines), jnp.float32)
+    jumps[...] = jnp.concatenate([jump_wide, pad], axis=1)
+    joined = jnp.zeros((count * wide, lines * narrow), jnp.float32)
+    for J in range(narrow):
+        part = [jumps[pl.ds(J * count + mode, wide, stride=span), :] for mode in range(count)]
+        joined = joined + exact(jnp.concatenate(part, axis=0)[:, :lines], t["join"][J])
+    wide_gain = []
+    for mode in range(count):
+        at, top = decay[2 * mode : 2 * mode + 1], decay[2 * mode + 1 : 2 * mode + 2]
+        wide_gain.append(top / (at * at + 2.0 * (1.0 + at) * t["angle"][...]))
+    wide_sine = t["wide_sine"][...]
+    shaped = exact(wide_sine, jnp.concatenate(wide_gain, axis=0) * exact(wide_sine, joined))
+    pad = jnp.zeros((wide, LANES - lines), jnp.float32)
+    for J in range(narrow):
+        part = exact_turned(shaped, t["join"][J])
+        for mode in range(count):
+            fluxes[pl.ds(J * count + mode, wide, stride=span), :] = jnp.concatenate(
+                [part[mode * wide : (mode + 1) * wide], pad], axis=1
+            )
+    padded_wide = fluxes[...]
+    flux_wide = padded_wide[:, :lines]
+    moved = []
+    for side in range(2):
+        value = by_mode(flux_wide, influence(t["box_modes_turned"], t["faces_turned"], side, False))
+        moved.append(alternate[:, :rows] * up(value, span) - value)
+    jump_narrow = jump_narrow + jnp.where(has_narrow, moved[0] - pltpu.roll(moved[1], count, 0), 0.0)
+    flux_narrow = glued(jump_narrow)
+    padded_high = up(padded_wide, span)
+    balanced = exact(t["balance"][...], (padded_high - padded_wide)[:, :rows])
+    level = exact(t["level_flux"][...], balanced) + exact(t["level_jump"][...], jump_narrow)
+    level = level + exact(t["level_wide"][...], joined[:, :rows])
+    flux_narrow = jnp.where(row_zero & (own_mode == 0) & holds_steady, balanced, flux_narrow)
+    rest = level[:, : LANES - 2 * rows]
+    return jnp.concatenate([padded_wide, padded_high, flux_narrow, up(flux_narrow, count), rest], axis=1)
+
+
+def exchange_kernel(wide_place_order, *refs):
+    wide, narrow = wide_place_order
+    names = len(FIXED)
+    wide_in, narrow_in = refs[:2]
+    sources = refs[2 : 2 + names]
+    gain_hbm, decay_hbm, modes_ref, wide_ref, narrow_ref, level_ref = refs[2 + names : 8 + names]
+    fixed = refs[8 + names : 8 + 2 * names]
+    gain, decay, near_a, near_b, far_a, far_b, near_c, far_c, jumps, fluxes = refs[8 + 2 * names : 18 + 2 * names]
+    table_sem, near_send, near_recv, far_send, far_recv, near_send2, near_recv2, far_send2, far_recv2 = refs[18 + 2 * names :]
+    lines, depth = wide_in.shape[1:]
+    rows = narrow_in.shape[1]
+    count = depth // (wide * narrow)
+    place = lax.axis_index("narrow") * wide + lax.axis_index("wide")
+    per_block = 8 // (2 * count)
+    own = [(gain_hbm.at[place], gain), (decay_hbm.at[lax.div(place, per_block)], decay)]
+    copies = start_all(list(zip(sources, fixed)) + own, table_sem)
+    gap = jnp.zeros((LANES - lines, depth), jnp.float32)
+    rest = jnp.zeros((LANES - 2 * rows, depth), jnp.float32)
+    values = jnp.concatenate([wide_in[0], gap, wide_in[1], gap, narrow_in[0], narrow_in[1], rest], axis=0).T
+    far_rows = wide * count
     for p in range(narrow):
-        first[p] = values[p * far_rows : (p + 1) * far_rows]
+        near_a[p] = values[p * far_rows : (p + 1) * far_rows]
     greet(wide, narrow)
-    trade("narrow", first, near, near_send, near_recv)
-    turn(near, turned)
-    trade("wide", turned, out_ref, far_send, far_recv)
-
-
-def scatter_kernel(in_ref, wide_ref, narrow_ref, level_ref, far, turned, near, near_send, near_recv, far_send, far_recv):
-    narrow = near.shape[0]
-    wide = far.shape[0]
-    greet(wide, narrow)
-    trade("wide", in_ref, far, far_send, far_recv)
-    turn(far, turned)
-    trade("narrow", turned, near, near_send, near_recv)
-    values = jnp.concatenate([near[p] for p in range(narrow)], axis=0).T
-    lines, rows = wide_ref.shape[1], narrow_ref.shape[1]
+    trade("narrow", near_a, near_b, near_send, near_recv)
+    turn(near_b, far_a)
+    trade("wide", far_a, far_b, far_send, far_recv)
+    for copy in copies:
+        copy.wait()
+    traces = jnp.concatenate([far_b[p] for p in range(wide)], axis=0)
+    here = lax.rem(place, per_block)
+    own_decay = decay[: 2 * count]
+    for p in range(1, per_block):
+        own_decay = jnp.where(here == p, decay[p * 2 * count : (p + 1) * 2 * count], own_decay)
+    table = dict(zip(FIXED, fixed))
+    out = interfaces(traces, table, gain[...], own_decay, modes_ref, place, jumps, fluxes, wide, narrow)
+    span = narrow * count
+    for p in range(wide):
+        far_a[p] = out[p * span : (p + 1) * span]
+    trade("wide", far_a, far_c, far_send2, far_recv2)
+    turn(far_c, near_a)
+    trade("narrow", near_a, near_c, near_send2, near_recv2)
+    values = jnp.concatenate([near_c[p] for p in range(narrow)], axis=0).T
     wide_ref[0] = values[:lines]
-    wide_ref[1] = values[lines : 2 * lines]
-    narrow_ref[0] = values[2 * lines : 2 * lines + rows]
-    narrow_ref[1] = values[2 * lines + rows : 2 * (lines + rows)]
-    level_ref[...] = values[2 * (lines + rows) : 2 * (lines + rows) + 8]
-
-
-def message_width(rows, lines):
-    return -(-(2 * (rows + lines) + 8) // LANES) * LANES
+    wide_ref[1] = values[LANES : LANES + lines]
+    narrow_ref[0] = values[2 * LANES : 2 * LANES + rows]
+    narrow_ref[1] = values[2 * LANES + rows : 2 * LANES + 2 * rows]
+    level_ref[...] = values[2 * (LANES + rows) : 2 * (LANES + rows) + 8]
+
+
+def start_all(pairs, sem):
+    copies = [pltpu.make_async_copy(source, target, sem.at[i]) for i, (source, target) in enumerate(pairs)]
+    for copy in copies:
+        copy.start()
+    return copies
 
 
 IN_VMEM = pl.BlockSpec(memory_space=pltpu.VMEM)
-
-
-def semaphores(wide, narrow):
-    return [pltpu.SemaphoreType.DMA((k,)) for k in (narrow, narrow, wide, wide)]
-
-
-def gather(wide_traces, narrow_traces, wide, narrow):
+IN_HBM = pl.BlockSpec(memory_space=pl.ANY)
+IN_SMEM = pl.BlockSpec(memory_space=pltpu.SMEM)
+
+
+def exchange(wide_traces, narrow_traces, wide, narrow):
     lines, depth = wide_traces.shape[1:]
     rows = narrow_traces.shape[1]
     count = depth // (wide * narrow)
-    width = message_width(rows, lines)
+    width = 3 * LANES
+    t = tables(rows, lines, depth, wide, narrow)
     near = (narrow, wide * count, width)
     far = (wide, narrow * count, width)
+    face_rows = (wide * narrow * count, LANES)
+    f32 = jnp.float32
+    fixed = [jnp.asarray(t[name]) for name in FIXED]
+    shapes = [v.shape for v in fixed] + [t["gain"].shape[1:], t["decay"].shape[1:]]
+    shapes += [near, near, far, far, near, far, face_rows, face_rows]
+    sems = [len(fixed) + 2, narrow, narrow, wide, wide, narrow, narrow, wide, wide]
     return pl.pallas_call(
-        gather_kernel,
-        out_shape=jax.ShapeDtypeStruct(far, jnp.float32),
-        in_specs=[IN_VMEM, IN_VMEM],
-        out_specs=IN_VMEM,
-        scratch_shapes=[pltpu.VMEM(v, jnp.float32) for v in (near, near, far)] + semaphores(wide, narrow),
-        compiler_params=pltpu.CompilerParams(collective_id=0, has_side_effects=True),
-    )(wide_traces, narrow_traces)
-
-
-def scatter(fluxes, rows, lines, depth):
-    wide, _, width = fluxes.shape
-    narrow = lax.axis_size("narrow")
-    count = depth // (wide * narrow)
-    near = (narrow, wide * count, width)
-    far = (wide, narrow * count, width)
-    f32 = jnp.float32
-    return pl.pallas_call(
-        scatter_kernel,
+        functools.partial(exchange_kernel, (wide, narrow)),
         out_shape=[
             jax.ShapeDtypeStruct((2, lines, depth), f32),
             jax.ShapeDtypeStruct((2, rows, depth), f32),
             jax.ShapeDtypeStruct((8, depth), f32),
         ],
-        in_specs=[IN_VMEM],
+        in_specs=[IN_VMEM, IN_VMEM] + [IN_HBM] * (len(fixed) + 2) + [IN_SMEM],
         out_specs=[IN_VMEM] * 3,
-        scratch_shapes=[pltpu.VMEM(v, f32) for v in (far, near, near)] + semaphores(wide, narrow),
-        compiler_params=pltpu.CompilerParams(collective_id=1, has_side_effects=True),
-    )(fluxes)
+        scratch_shapes=[pltpu.VMEM(v, f32) for v in shapes] + [pltpu.SemaphoreType.DMA((k,)) for k in sems],
+        compiler_params=pltpu.CompilerParams(
+            collective_id=0, has_side_effects=True, vmem_limit_bytes=VMEM_LIMIT
+        ),
+    )(
+        wide_traces,
+        narrow_traces,
+        *fixed,
+        jnp.asarray(t["gain"]),
+        jnp.asarray(t["decay"]),
+        jnp.asarray(modes(depth), f32),
+    )
 
 
 VMEM_LIMIT = 60 * 2**20
@@ -485,102 +652,12 @@
     )
 
 
-def own(table, place, count):
-    return lax.dynamic_slice_in_dim(jnp.asarray(table), place * count, count, axis=0)
-
-
-def alternate(length):
-    return jnp.asarray(signs(length), jnp.float32)
-
-
-def eigen(index, count):
-    half_sine = jnp.sin(index.astype(jnp.float32) * (math.pi / (2 * count)))
-    return 4.0 * half_sine * half_sine
-
-
-def interfaces(traces, t, place, rows, lines, depth, wide, narrow):
-    count = traces.shape[1] // narrow
-    traces = traces.reshape(wide, narrow, count, -1)
-    traces = jnp.transpose(traces, (2, 0, 1, 3))
-    cut = [lines, 2 * lines, 2 * lines + rows, 2 * (lines + rows)]
-    wide_low, wide_high, narrow_low, narrow_high, _ = jnp.split(traces, cut, axis=-1)
-    jump_wide = wide_low[:, 1:] - wide_high[:, :-1]
-    jump_narrow = narrow_low[:, :, 1:] - narrow_high[:, :, :-1]
-    depth_place = place * count + jnp.arange(count)
-    steady = depth_place == 0
-    depth_part = eigen(depth_place, depth)
-    row_zero = jnp.arange(rows) == 0
-    line_zero = jnp.arange(lines) == 0
-    last = jnp.einsum("mjl,rmk->rjlk", t["narrow_sines"], own(t["narrow_gain"], place, count), precision=HIGHEST)
-    first = jnp.where(
-        steady[:, None, None, None] & row_zero, jnp.asarray(t["narrow_steady"])[None, :, :, None], last
-    )
-    eig = (
-        depth_part[:, None, None]
-        + jnp.asarray(modes(rows), jnp.float32)[:, None]
-        + jnp.asarray(modes(lines), jnp.float32)[None, :]
-    )
-    faces = jnp.asarray(face(rows)[:, None] * face(lines)[None, :], jnp.float32)
-    steady_row = steady[:, None, None] & row_zero[:, None]
-    zero_mode = steady_row & line_zero
-    weight = faces / jnp.where(zero_mode, 1.0, eig)
-    weight_first = jnp.where(steady_row & ~line_zero, 0.0, weight)
-    weight_last = jnp.swapaxes(jnp.where(zero_mode, 0.0, weight), 1, 2)
-    to_wide = jnp.stack([weight_first, weight_first * alternate(rows)[:, None]], axis=2)
-    to_narrow = jnp.stack([weight_last, weight_last * alternate(lines)[:, None]], axis=2)
-    shift = depth_part[:, None] + jnp.asarray(modes(lines * narrow), jnp.float32)[None, :]
-    decay = own(t["wide_decay"], place, count)
-    top = -jnp.sqrt(shift / (4.0 + shift)) * decay * (2.0 + decay)
-    top = top[:, None, :]
-    decay = decay[:, None, :]
-    bottom = decay * decay + 2.0 * (1.0 + decay) * jnp.asarray(t["wide_angle"])[None, :, None]
-    wide_gain = top / bottom
-    flux = jnp.sum(first[:, None] * jump_narrow[:, :, None], axis=3)
-    moved = jnp.einsum("rIjk,rksb->rsIjb", flux, to_wide, precision=HIGHEST)
-    edge = [(0, 0)] * 3
-    moved = jnp.pad(moved, edge + [(0, 1), (0, 0)]) * alternate(lines) - jnp.pad(moved, edge + [(1, 0), (0, 0)])
-    jump_wide = jump_wide + moved[:, 0, 1:] - moved[:, 1, :-1]
-    jump_wide = jump_wide.reshape(count, wide - 1, narrow * lines)
-    joined = jnp.einsum("riy,qy->riq", jump_wide, t["join"], precision=HIGHEST)
-    shaped = jnp.einsum("mi,riq->rmq", t["wide_sine"], joined, precision=HIGHEST)
-    shaped = shaped * wide_gain
-    shaped = jnp.einsum("mi,rmq->riq", t["wide_sine"], shaped, precision=HIGHEST)
-    flux_wide = jnp.einsum("riq,qy->riy", shaped, t["join"], precision=HIGHEST)
-    flux_wide = flux_wide.reshape(count, wide - 1, narrow, lines)
-    flux_wide = jnp.pad(flux_wide, [(0, 0), (1, 1), (0, 0), (0, 0)])
-    moved = jnp.einsum("riJb,rbsk->rsiJk", flux_wide, to_narrow, precision=HIGHEST)
-    moved = moved[:, :, 1:] * alternate(rows) - moved[:, :, :-1]
-    jump_narrow = jump_narrow + moved[:, 0, :, 1:] - moved[:, 1, :, :-1]
-    flux_narrow = jnp.sum(last[:, None] * jump_narrow[:, :, None], axis=3)
-    mean_flux = flux_wide[0, 1:, :, 0] - flux_wide[0, :-1, :, 0]
-    balanced = jnp.einsum("IJ,Jj->Ij", mean_flux, t["balance"], precision=HIGHEST)
-    level = jnp.einsum("Ij,jJ->IJ", balanced, t["level_of_flux"], precision=HIGHEST)
-    level = level + jnp.einsum("Ij,jJ->IJ", jump_narrow[0, :, :, 0], t["level_of_jump"], precision=HIGHEST)
-    level = level + jnp.einsum("Ii,i->I", t["wide_levels"], joined[0, :, 0], precision=HIGHEST)[:, None]
-    flux_narrow = jnp.where(
-        steady[:, None, None, None] & row_zero, balanced[None, :, :, None], flux_narrow
-    )
-    flux_narrow = jnp.pad(flux_narrow, [(0, 0), (0, 0), (1, 1), (0, 0)])
-    level = jnp.broadcast_to(level[None, :, :, None], (count, wide, narrow, message_width(rows, lines) - 2 * (rows + lines)))
-    out = jnp.concatenate(
-        [flux_wide[:, :-1], flux_wide[:, 1:], flux_narrow[:, :, :-1], flux_narrow[:, :, 1:], level], axis=-1
-    )
-    out = jnp.transpose(out, (1, 2, 0, 3))
-    return out.reshape(wide, narrow * count, -1)
-
-
 def shards(slope_first, slope_second, slope_third):
     rows, lines, depth = slope_first.shape
     wide = lax.axis_size("wide")
     narrow = lax.axis_size("narrow")
-    wide_place = lax.axis_index("wide")
-    narrow_place = lax.axis_index("narrow")
-    place = narrow_place * wide + wide_place
-    t = tables(rows, lines, depth, wide, narrow)
     spectrum, wide_traces, narrow_traces = forward(slope_first, slope_second, slope_third)
-    traces = gather(wide_traces, narrow_traces, wide, narrow)
-    fluxes = interfaces(traces, t, place, rows, lines, depth, wide, narrow)
-    wide_flux, narrow_flux, level = scatter(fluxes, rows, lines, depth)
+    wide_flux, narrow_flux, level = exchange(wide_traces, narrow_traces, wide, narrow)
     return inverse(spectrum, wide_flux, narrow_flux, level)
 
 

time: 89.2 us -> 77.3 us (0.87)
  matrix products: 6.65 us -> 0 us
  other arithmetic: 4.13 us -> 0 us
  local copies, waits for them, and re-layouts: 3.6 us -> 0 us
  Pallas kernels: 73.8 us -> 77 us
    dot_general x11 -> x0, matrix products: 6.65 us -> none  [the longest x1 2.22 us: interfaces(): joined = jnp.einsum('riy,qy->riq', jump_wide, t['join'], precision=HIGHEST)]
    pallas_call x2 -> x1, Pallas kernels: 44.4 us -> 47.6 us  [exchange(): pl.pallas_call(functools.partial(exchange_kernel, (wide, narrow)), out_sh...]
    reshape x7 -> x0, local copies, waits for them, and re-layouts: 2.65 us -> none  [the longest x2 1.35 us: interfaces(): traces = traces.reshape(wide, narrow, count, -1)]
    select_n x3 -> x0, other arithmetic: 1.76 us -> none  [the longest x1 0.84 us: interfaces(): weight_last = jnp.swapaxes(jnp.where(zero_mode, 0.0, weight), 1, 2)]
where the time goes in v4:
time: 77.3 us; the launch traced here: 77 us
  Pallas kernels  77 us (100%)
    pallas_call x1, Pallas kernels, exchange(): pl.pallas_call(functools.partial(exchange_kernel, (wide, narrow)), out_sh...  47.6 us
    pallas_call x1, Pallas kernels, forward(): pl.pallas_call(functools.partial(forward_kernel, steps), grid=(steps + gr...  16.4 us
    pallas_call x1, Pallas kernels, inverse(): pl.pallas_call(functools.partial(inverse_kernel, groups), grid=(steps + g...  13 us

profile of v4, /device:TPU:1, one launch (start us, length us, event | category | flops | bytes accessed | tf_op | source)
XLA Modules:
  0.0 77.0 jit_solution(13640033189796204418)
XLA Ops:
  0.0 16.4 %shard_map.334 = (f32[96,48,256]{2,1,0:T(8,128)}, f32[2,96,256]{2,1,0:T(8,128)}, f32[2,48,256]{2,1,0:T(8,128)}) custom-call(f32[48,96,256]{2,1,0:T(8,128)} %first_ref.1, f32[48,96,256]{2,1,0:T(8,128)} %second_ref.1, f32[48,96,256]{2,1,0:T(8,128)} %third_ref.1, bf16[256,256]{1,0:T(8,128)(2,1)} %constant.58.clone.depth_high_ref, ...), custom_call_target="tpu_custom_call" | custom-call | tf_op jit(solution)/shard_map/pallas_call | solution.py:591
  16.4 47.6 %shard_map.335 = (f32[2,96,256]{2,1,0:T(8,128)}, f32[2,48,256]{2,1,0:T(8,128)}, f32[8,256]{1,0:T(8,128)}) custom-call(f32[2,96,256]{2,1,0:T(8,128)} %get-tuple-element.12.refs_0_, f32[2,48,256]{2,1,0:T(8,128)} %get-tuple-element.13.refs_1_, f32[256,256]{1,0:T(8,128)} %constant.66.clone.refs_2_, f32[256,256]{1,0:T(8,128)} %constant.67.clone.refs_3_, ...), custom_call_target="tpu_custom_call" | custom-call | tf_op jit(solution)/shard_map/pallas_call | solution.py:532
  64.0 13.0 %shard_map.336 = f32[48,96,256]{2,1,0:T(8,128)} custom-call(f32[96,48,256]{2,1,0:T(8,128)} %get-tuple-element.11.spectrum_ref, f32[2,96,256]{2,1,0:T(8,128)} %get-tuple-element.14.wide_ref, f32[2,48,256]{2,1,0:T(8,128)} %get-tuple-element.15.narrow_ref, f32[8,256]{1,0:T(8,128)} %get-tuple-element.16.level_ref, ...), custom_call_target="tpu_custom_call" | custom-call | tf_op jit(solution)/shard_map/pallas_call | solution.py:628

commit v5 on v4

--- a/solution.py
+++ b/solution.py
@@ -103,7 +103,9 @@
     gain = gain.reshape(wide * narrow, count, narrow, rows).swapaxes(1, 2)
     t["gain"] = lane_padded(gain.reshape(wide * narrow, narrow * count, rows))
     full = cosine_matrix(lines * narrow).reshape(lines * narrow, narrow, lines)
-    t["join"] = np.einsum("qJn,kn->Jkq", full, cosine_matrix(lines))
+    join = np.einsum("qJn,kn->Jkq", full, cosine_matrix(lines))
+    t["join_high"], t["join_low"] = halves(join)
+    t["part_high"], t["part_low"] = halves(np.swapaxes(join, 1, 2))
     shift = depth_modes[:, None] + modes(lines * narrow)[None, :]
     decay = np.expm1(-exponent(shift) * rows)
     top = -np.sqrt(shift / (4.0 + shift)) * decay * (2.0 + decay)
@@ -118,7 +120,10 @@
     t["box_modes_turned"] = t["box_modes"].T
     t["faces_turned"] = np.stack([both.T, both.T * signs(lines)[:, None]])
     t["alternate"] = np.broadcast_to(signs(LANES)[None, :], (8, LANES))
-    return {name: np.ascontiguousarray(value, dtype=np.float32) for name, value in t.items()}
+    return {
+        name: np.ascontiguousarray(value, dtype=jnp.bfloat16 if name[:4] in ("join", "part") else np.float32)
+        for name, value in t.items()
+    }
 
 
 FIXED = (
@@ -128,7 +133,10 @@
     "level_flux",
     "level_jump",
     "level_wide",
-    "join",
+    "join_high",
+    "join_low",
+    "part_high",
+    "part_low",
     "wide_sine",
     "angle",
     "box_modes",
@@ -257,9 +265,9 @@
             closed = closed * line_face_ref[line]
             narrow_low = narrow_low + closed
             narrow_high = narrow_high + closed if i % 2 == 0 else narrow_high - closed
-        wide_ref[0] = jnp.concatenate(lows, axis=0)
         here = pl.ds(pl.multiple_of((step - steps) * group, 8), group)
-        wide_ref[1] = jnp.concatenate(highs, axis=0) + wide_face[here, :]
+        wide_ref[0, here, :] = jnp.concatenate(lows, axis=0)
+        wide_ref[1, here, :] = jnp.concatenate(highs, axis=0) + wide_face[here, :]
         narrow_ref[0] = narrow_low
         narrow_ref[1] = narrow_high
 
@@ -318,7 +326,6 @@
         pl.semaphore_signal(barrier, inc=1, device_id=(w, lax.rem(n + d, narrow)), device_id_type=MESH)
     for d in range(1, wide):
         pl.semaphore_signal(barrier, inc=1, device_id=(lax.rem(w + d, wide), n), device_id_type=MESH)
-    pl.semaphore_wait(barrier, wide + narrow - 2)
 
 
 def trade(axis, source, target, send, recv):
@@ -358,12 +365,6 @@
     return jnp.dot(a, b, precision=HIGHEST, preferred_element_type=jnp.float32)
 
 
-def exact_turned(a, b):
-    return lax.dot_general(
-        a, b, (((1,), (1,)), ((), ())), precision=HIGHEST, preferred_element_type=jnp.float32
-    )
-
-
 def interfaces(traces, t, gain, decay, modes_ref, place, jumps, fluxes, wide, narrow):
     total = traces.shape[0]
     count = total // (wide * narrow)
@@ -423,7 +424,9 @@
     joined = jnp.zeros((count * wide, lines * narrow), jnp.float32)
     for J in range(narrow):
         part = [jumps[pl.ds(J * count + mode, wide, stride=span), :] for mode in range(count)]
-        joined = joined + exact(jnp.concatenate(part, axis=0)[:, :lines], t["join"][J])
+        joined = joined + from_right(
+            jnp.concatenate(part, axis=0)[:, :lines], t["join_high"][J], t["join_low"][J]
+        )
     wide_gain = []
     for mode in range(count):
         at, top = decay[2 * mode : 2 * mode + 1], decay[2 * mode + 1 : 2 * mode + 2]
@@ -432,7 +435,7 @@
     shaped = exact(wide_sine, jnp.concatenate(wide_gain, axis=0) * exact(wide_sine, joined))
     pad = jnp.zeros((wide, LANES - lines), jnp.float32)
     for J in range(narrow):
-        part = exact_turned(shaped, t["join"][J])
+        part = from_right(shaped, t["part_high"][J], t["part_low"][J])
         for mode in range(count):
             fluxes[pl.ds(J * count + mode, wide, stride=span), :] = jnp.concatenate(
                 [part[mode * wide : (mode + 1) * wide], pad], axis=1
@@ -454,102 +457,75 @@
     return jnp.concatenate([padded_wide, padded_high, flux_narrow, up(flux_narrow, count), rest], axis=1)
 
 
-def exchange_kernel(wide_place_order, *refs):
-    wide, narrow = wide_place_order
+def forward_exchange_kernel(steps, groups, wide, narrow, *refs):
+    step = pl.program_id(0)
     names = len(FIXED)
-    wide_in, narrow_in = refs[:2]
-    sources = refs[2 : 2 + names]
-    gain_hbm, decay_hbm, modes_ref, wide_ref, narrow_ref, level_ref = refs[2 + names : 8 + names]
-    fixed = refs[8 + names : 8 + 2 * names]
-    gain, decay, near_a, near_b, far_a, far_b, near_c, far_c, jumps, fluxes = refs[8 + 2 * names : 18 + 2 * names]
-    table_sem, near_send, near_recv, far_send, far_recv, near_send2, near_recv2, far_send2, far_recv2 = refs[18 + 2 * names :]
+    box_in, refs = refs[:11], refs[11:]
+    sources, gain_hbm, decay_hbm, modes_ref = refs[:names], refs[names], refs[names + 1], refs[names + 2]
+    spectrum_ref, wide_ref, narrow_ref, level_ref = refs[names + 3 : names + 7]
+    refs = refs[names + 7 :]
+    carry, held, wide_face, narrow_face, wide_in, narrow_in = refs[:6]
+    fixed, refs = refs[6 : 6 + names], refs[6 + names :]
+    gain, decay, near_a, near_b, far_a, far_b, near_c, far_c, jumps, fluxes = refs[:10]
+    table_sem, near_send, near_recv, far_send, far_recv, near_send2, near_recv2, far_send2, far_recv2 = refs[10:]
     lines, depth = wide_in.shape[1:]
     rows = narrow_in.shape[1]
     count = depth // (wide * narrow)
     place = lax.axis_index("narrow") * wide + lax.axis_index("wide")
     per_block = 8 // (2 * count)
     own = [(gain_hbm.at[place], gain), (decay_hbm.at[lax.div(place, per_block)], decay)]
-    copies = start_all(list(zip(sources, fixed)) + own, table_sem)
-    gap = jnp.zeros((LANES - lines, depth), jnp.float32)
-    rest = jnp.zeros((LANES - 2 * rows, depth), jnp.float32)
-    values = jnp.concatenate([wide_in[0], gap, wide_in[1], gap, narrow_in[0], narrow_in[1], rest], axis=0).T
-    far_rows = wide * count
-    for p in range(narrow):
-        near_a[p] = values[p * far_rows : (p + 1) * far_rows]
-    greet(wide, narrow)
-    trade("narrow", near_a, near_b, near_send, near_recv)
-    turn(near_b, far_a)
-    trade("wide", far_a, far_b, far_send, far_recv)
-    for copy in copies:
-        copy.wait()
-    traces = jnp.concatenate([far_b[p] for p in range(wide)], axis=0)
-    here = lax.rem(place, per_block)
-    own_decay = decay[: 2 * count]
-    for p in range(1, per_block):
-        own_decay = jnp.where(here == p, decay[p * 2 * count : (p + 1) * 2 * count], own_decay)
-    table = dict(zip(FIXED, fixed))
-    out = interfaces(traces, table, gain[...], own_decay, modes_ref, place, jumps, fluxes, wide, narrow)
-    span = narrow * count
-    for p in range(wide):
-        far_a[p] = out[p * span : (p + 1) * span]
-    trade("wide", far_a, far_c, far_send2, far_recv2)
-    turn(far_c, near_a)
-    trade("narrow", near_a, near_c, near_send2, near_recv2)
-    values = jnp.concatenate([near_c[p] for p in range(narrow)], axis=0).T
-    wide_ref[0] = values[:lines]
-    wide_ref[1] = values[LANES : LANES + lines]
-    narrow_ref[0] = values[2 * LANES : 2 * LANES + rows]
-    narrow_ref[1] = values[2 * LANES + rows : 2 * LANES + 2 * rows]
-    level_ref[...] = values[2 * (LANES + rows) : 2 * (LANES + rows) + 8]
-
-
-def start_all(pairs, sem):
-    copies = [pltpu.make_async_copy(source, target, sem.at[i]) for i, (source, target) in enumerate(pairs)]
-    for copy in copies:
-        copy.start()
-    return copies
+    pairs = list(zip(sources, fixed)) + own
+
+    @pl.when(step == 0)
+    def _():
+        greet(wide, narrow)
+        for copy in prepared(pairs, table_sem):
+            copy.start()
+
+    forward_kernel(steps, *box_in, spectrum_ref, wide_in, narrow_in, carry, held, wide_face, narrow_face)
+
+    @pl.when(step == steps + groups - 1)
+    def _():
+        gap = jnp.zeros((LANES - lines, depth), jnp.float32)
+        rest = jnp.zeros((LANES - 2 * rows, depth), jnp.float32)
+        values = jnp.concatenate([wide_in[0], gap, wide_in[1], gap, narrow_in[0], narrow_in[1], rest], axis=0).T
+        far_rows = wide * count
+        for p in range(narrow):
+            near_a[p] = values[p * far_rows : (p + 1) * far_rows]
+        pl.semaphore_wait(pltpu.get_barrier_semaphore(), wide + narrow - 2)
+        trade("narrow", near_a, near_b, near_send, near_recv)
+        turn(near_b, far_a)
+        trade("wide", far_a, far_b, far_send, far_recv)
+        for copy in prepared(pairs, table_sem):
+            copy.wait()
+        traces = jnp.concatenate([far_b[p] for p in range(wide)], axis=0)
+        here = lax.rem(place, per_block)
+        own_decay = decay[: 2 * count]
+        for p in range(1, per_block):
+            own_decay = jnp.where(here == p, decay[p * 2 * count : (p + 1) * 2 * count], own_decay)
+        table = dict(zip(FIXED, fixed))
+        out = interfaces(traces, table, gain[...], own_decay, modes_ref, place, jumps, fluxes, wide, narrow)
+        span = narrow * count
+        for p in range(wide):
+            far_a[p] = out[p * span : (p + 1) * span]
+        trade("wide", far_a, far_c, far_send2, far_recv2)
+        turn(far_c, near_a)
+        trade("narrow", near_a, near_c, near_send2, near_recv2)
+        values = jnp.concatenate([near_c[p] for p in range(narrow)], axis=0).T
+        wide_ref[0] = values[:lines]
+        wide_ref[1] = values[LANES : LANES + lines]
+        narrow_ref[0] = values[2 * LANES : 2 * LANES + rows]
+        narrow_ref[1] = values[2 * LANES + rows : 2 * LANES + 2 * rows]
+        level_ref[...] = values[2 * (LANES + rows) : 2 * (LANES + rows) + 8]
+
+
+def prepared(pairs, sem):
+    return [pltpu.make_async_copy(source, target, sem.at[i]) for i, (source, target) in enumerate(pairs)]
 
 
 IN_VMEM = pl.BlockSpec(memory_space=pltpu.VMEM)
 IN_HBM = pl.BlockSpec(memory_space=pl.ANY)
 IN_SMEM = pl.BlockSpec(memory_space=pltpu.SMEM)
-
-
-def exchange(wide_traces, narrow_traces, wide, narrow):
-    lines, depth = wide_traces.shape[1:]
-    rows = narrow_traces.shape[1]
-    count = depth // (wide * narrow)
-    width = 3 * LANES
-    t = tables(rows, lines, depth, wide, narrow)
-    near = (narrow, wide * count, width)
-    far = (wide, narrow * count, width)
-    face_rows = (wide * narrow * count, LANES)
-    f32 = jnp.float32
-    fixed = [jnp.asarray(t[name]) for name in FIXED]
-    shapes = [v.shape for v in fixed] + [t["gain"].shape[1:], t["decay"].shape[1:]]
-    shapes += [near, near, far, far, near, far, face_rows, face_rows]
-    sems = [len(fixed) + 2, narrow, narrow, wide, wide, narrow, narrow, wide, wide]
-    return pl.pallas_call(
-        functools.partial(exchange_kernel, (wide, narrow)),
-        out_shape=[
-            jax.ShapeDtypeStruct((2, lines, depth), f32),
-            jax.ShapeDtypeStruct((2, rows, depth), f32),
-            jax.ShapeDtypeStruct((8, depth), f32),
-        ],
-        in_specs=[IN_VMEM, IN_VMEM] + [IN_HBM] * (len(fixed) + 2) + [IN_SMEM],
-        out_specs=[IN_VMEM] * 3,
-        scratch_shapes=[pltpu.VMEM(v, f32) for v in shapes] + [pltpu.SemaphoreType.DMA((k,)) for k in sems],
-        compiler_params=pltpu.CompilerParams(
-            collective_id=0, has_side_effects=True, vmem_limit_bytes=VMEM_LIMIT
-        ),
-    )(
-        wide_traces,
-        narrow_traces,
-        *fixed,
-        jnp.asarray(t["gain"]),
-        jnp.asarray(t["decay"]),
-        jnp.asarray(modes(depth), f32),
-    )
 
 
 VMEM_LIMIT = 60 * 2**20
@@ -582,33 +558,55 @@
     ]
 
 
-def forward(first, second, third):
+def forward_exchange(first, second, third, wide, narrow):
     rows, lines, depth = first.shape
     steps, groups = rows // BLOCK, lines // GROUP
+    count = depth // (wide * narrow)
     slab = pl.BlockSpec((BLOCK, lines, depth), lambda s: (jnp.minimum(s, steps - 1), 0, 0))
     depth_high, depth_low = halves(cosine_matrix(depth).T)
+    t = tables(rows, lines, depth, wide, narrow)
+    width = 3 * LANES
+    near = (narrow, wide * count, width)
+    far = (wide, narrow * count, width)
+    face_rows = (wide * narrow * count, LANES)
     f32 = jnp.float32
+    fixed = [jnp.asarray(t[name]) for name in FIXED]
+    box_shapes = [
+        (lines, depth),
+        (depth // LANES, rows * lines, LANES),
+        (lines, depth),
+        (rows, depth),
+        (2, lines, depth),
+        (2, rows, depth),
+    ]
+    shapes = [t["gain"].shape[1:], t["decay"].shape[1:], near, near, far, far, near, far, face_rows, face_rows]
+    sems = [len(fixed) + 2, narrow, narrow, wide, wide, narrow, narrow, wide, wide]
     return pl.pallas_call(
-        functools.partial(forward_kernel, steps),
+        functools.partial(forward_exchange_kernel, steps, groups, wide, narrow),
         grid=(steps + groups,),
         out_shape=[
             jax.ShapeDtypeStruct((lines, rows, depth), f32),
             jax.ShapeDtypeStruct((2, lines, depth), f32),
             jax.ShapeDtypeStruct((2, rows, depth), f32),
+            jax.ShapeDtypeStruct((8, depth), f32),
         ],
-        in_specs=[slab, slab, slab] + table_specs(rows, lines, depth),
+        in_specs=[slab, slab, slab]
+        + table_specs(rows, lines, depth)
+        + [IN_HBM] * (len(fixed) + 2)
+        + [IN_SMEM],
         out_specs=[
             pl.BlockSpec((GROUP, rows, depth), lambda s: (jnp.maximum(s - steps, 0), 0, 0)),
-            pl.BlockSpec((2, GROUP, depth), lambda s: (0, jnp.maximum(s - steps, 0), 0)),
+            whole(2, lines, depth),
             whole(2, rows, depth),
+            whole(8, depth),
         ],
-        scratch_shapes=[
-            pltpu.VMEM((lines, depth), f32),
-            pltpu.VMEM((depth // LANES, rows * lines, LANES), f32),
-            pltpu.VMEM((lines, depth), f32),
-            pltpu.VMEM((rows, depth), f32),
-        ],
-        compiler_params=pltpu.CompilerParams(vmem_limit_bytes=VMEM_LIMIT),
+        scratch_shapes=[pltpu.VMEM(v, f32) for v in box_shapes]
+        + [pltpu.VMEM(v.shape, v.dtype) for v in fixed]
+        + [pltpu.VMEM(v, f32) for v in shapes]
+        + [pltpu.SemaphoreType.DMA((k,)) for k in sems],
+        compiler_params=pltpu.CompilerParams(
+            collective_id=0, has_side_effects=True, vmem_limit_bytes=VMEM_LIMIT
+        ),
     )(
         first,
         second,
@@ -618,6 +616,10 @@
         jnp.asarray(left_table(cosine_matrix(lines))),
         jnp.asarray(left_table(cosine_matrix(rows))),
         *box_tables(rows, lines, depth),
+        *fixed,
+        jnp.asarray(t["gain"]),
+        jnp.asarray(t["decay"]),
+        jnp.asarray(modes(depth), f32),
     )
 
 
@@ -656,8 +658,7 @@
     rows, lines, depth = slope_first.shape
     wide = lax.axis_size("wide")
     narrow = lax.axis_size("narrow")
-    spectrum, wide_traces, narrow_traces = forward(slope_first, slope_second, slope_third)
-    wide_flux, narrow_flux, level = exchange(wide_traces, narrow_traces, wide, narrow)
+    spectrum, wide_flux, narrow_flux, level = forward_exchange(slope_first, slope_second, slope_third, wide, narrow)
     return inverse(spectrum, wide_flux, narrow_flux, level)
 
 

time: 77.3 us -> 69.8 us (0.903)
  Pallas kernels: 77 us -> 69.5 us
    pallas_call x2 -> x1, Pallas kernels: 64 us -> 56.5 us  [forward_exchange(): pl.pallas_call(functools.partial(forward_exchange_kernel, steps, groups,...]
where the time goes in v5:
time: 69.8 us; the launch traced here: 69.6 us
  Pallas kernels  69.5 us (100%)
    pallas_call x1, Pallas kernels, forward_exchange(): pl.pallas_call(functools.partial(forward_exchange_kernel, steps, groups,...  56.5 us
    pallas_call x1, Pallas kernels, inverse(): pl.pallas_call(functools.partial(inverse_kernel, groups), grid=(steps + g...  13 us

profile of v5, /device:TPU:1, one launch (start us, length us, event | category | flops | bytes accessed | tf_op | source)
XLA Modules:
  0.0 69.6 jit_solution(10323598483421187142)
XLA Ops:
  0.0 56.5 %shard_map.361 = (f32[96,48,256]{2,1,0:T(8,128)}, f32[2,96,256]{2,1,0:T(8,128)}, f32[2,48,256]{2,1,0:T(8,128)}, f32[8,256]{1,0:T(8,128)}) custom-call(f32[48,96,256]{2,1,0:T(8,128)} %refs_0_.1, f32[48,96,256]{2,1,0:T(8,128)} %refs_1_.1, f32[48,96,256]{2,1,0:T(8,128)} %refs_2_.1, bf16[256,256]{1,0:T(8,128)(2,1)} %constant.81.clone.refs_3_, ...), custom_call_target="tpu_custom_call" | custom-call | tf_op jit(solution)/shard_map/pallas_call | solution.py:584
  56.5 13.0 %shard_map.362 = f32[48,96,256]{2,1,0:T(8,128)} custom-call(f32[96,48,256]{2,1,0:T(8,128)} %get-tuple-element.9.spectrum_ref, f32[2,96,256]{2,1,0:T(8,128)} %get-tuple-element.10.wide_ref, f32[2,48,256]{2,1,0:T(8,128)} %get-tuple-element.11.narrow_ref, f32[8,256]{1,0:T(8,128)} %get-tuple-element.12.level_ref, ...), custom_call_target="tpu_custom_call" | custom-call | tf_op jit(solution)/shard_map/pallas_call | solution.py:630

commit v6 on v5

--- a/solution.py
+++ b/solution.py
@@ -365,6 +365,12 @@
     return jnp.dot(a, b, precision=HIGHEST, preferred_element_type=jnp.float32)
 
 
+def close(a, b):
+    a_high, a_low = split(a)
+    b_high, b_low = split(b)
+    return dot(a_high, b_high) + dot(a_low, b_high) + dot(a_high, b_low)
+
+
 def interfaces(traces, t, gain, decay, modes_ref, place, jumps, fluxes, wide, narrow):
     total = traces.shape[0]
     count = total // (wide * narrow)
@@ -380,9 +386,9 @@
         return pltpu.roll(x, total - by, 0)
 
     def by_mode(x, weights):
-        out = exact(x, weights[0])
+        out = close(x, weights[0])
         for mode in range(1, count):
-            out = jnp.where(own_mode == mode, exact(x, weights[mode]), out)
+            out = jnp.where(own_mode == mode, close(x, weights[mode]), out)
         return out
 
     def influence(box_modes, faces, side, first):
@@ -408,11 +414,11 @@
     sine = t["sine"][...]
 
     def glued(jump):
-        return exact(sine, gain * exact(sine, jump))
+        return close(sine, gain * close(sine, jump))
 
     row_zero = lax.broadcasted_iota(jnp.int32, (total, rows), 1) == 0
     flux = glued(jump_narrow)
-    steady = exact(t["steady"][...], jump_narrow)
+    steady = close(t["steady"][...], jump_narrow)
     flux = flux + jnp.where(row_zero & holds_steady, steady, 0.0)
     moved = []
     for side in range(2):
@@ -432,7 +438,7 @@
         at, top = decay[2 * mode : 2 * mode + 1], decay[2 * mode + 1 : 2 * mode + 2]
         wide_gain.append(top / (at * at + 2.0 * (1.0 + at) * t["angle"][...]))
     wide_sine = t["wide_sine"][...]
-    shaped = exact(wide_sine, jnp.concatenate(wide_gain, axis=0) * exact(wide_sine, joined))
+    shaped = close(wide_sine, jnp.concatenate(wide_gain, axis=0) * close(wide_sine, joined))
     pad = jnp.zeros((wide, LANES - lines), jnp.float32)
     for J in range(narrow):
         part = from_right(shaped, t["part_high"][J], t["part_low"][J])

time: 69.8 us -> 68.8 us (0.986)
  Pallas kernels: 69.5 us -> 68.6 us
    pallas_call x1, Pallas kernels: 56.5 us -> 55.5 us  [forward_exchange(): pl.pallas_call(functools.partial(forward_exchange_kernel, steps, groups,...]
where the time goes in v6:
time: 68.8 us; the launch traced here: 68.6 us
  Pallas kernels  68.6 us (100%)
    pallas_call x1, Pallas kernels, forward_exchange(): pl.pallas_call(functools.partial(forward_exchange_kernel, steps, groups,...  55.5 us
    pallas_call x1, Pallas kernels, inverse(): pl.pallas_call(functools.partial(inverse_kernel, groups), grid=(steps + g...  13 us

profile of v6, /device:TPU:1, one launch (start us, length us, event | category | flops | bytes accessed | tf_op | source)
XLA Modules:
  0.0 68.6 jit_solution(12795724586234759410)
XLA Ops:
  0.0 55.5 %shard_map.361 = (f32[96,48,256]{2,1,0:T(8,128)}, f32[2,96,256]{2,1,0:T(8,128)}, f32[2,48,256]{2,1,0:T(8,128)}, f32[8,256]{1,0:T(8,128)}) custom-call(f32[48,96,256]{2,1,0:T(8,128)} %refs_0_.1, f32[48,96,256]{2,1,0:T(8,128)} %refs_1_.1, f32[48,96,256]{2,1,0:T(8,128)} %refs_2_.1, bf16[256,256]{1,0:T(8,128)(2,1)} %constant.81.clone.refs_3_, ...), custom_call_target="tpu_custom_call" | custom-call | tf_op jit(solution)/shard_map/pallas_call | solution.py:590
  55.5 13.0 %shard_map.362 = f32[48,96,256]{2,1,0:T(8,128)} custom-call(f32[96,48,256]{2,1,0:T(8,128)} %get-tuple-element.9.spectrum_ref, f32[2,96,256]{2,1,0:T(8,128)} %get-tuple-element.10.wide_ref, f32[2,48,256]{2,1,0:T(8,128)} %get-tuple-element.11.narrow_ref, f32[8,256]{1,0:T(8,128)} %get-tuple-element.12.level_ref, ...), custom_call_target="tpu_custom_call" | custom-call | tf_op jit(solution)/shard_map/pallas_call | solution.py:636

commit v7 on v6

--- a/solution.py
+++ b/solution.py
@@ -8,8 +8,6 @@
 from jax.experimental import pallas as pl
 from jax.experimental.pallas import tpu as pltpu
 from jax.sharding import PartitionSpec as P
-
-HIGHEST = lax.Precision.HIGHEST
 
 
 LANES = 128
@@ -361,10 +359,6 @@
             target[b, a * count : (a + 1) * count, :] = source[a, b * count : (b + 1) * count, :]
 
 
-def exact(a, b):
-    return jnp.dot(a, b, precision=HIGHEST, preferred_element_type=jnp.float32)
-
-
 def close(a, b):
     a_high, a_low = split(a)
     b_high, b_low = split(b)
@@ -455,9 +449,9 @@
     jump_narrow = jump_narrow + jnp.where(has_narrow, moved[0] - pltpu.roll(moved[1], count, 0), 0.0)
     flux_narrow = glued(jump_narrow)
     padded_high = up(padded_wide, span)
-    balanced = exact(t["balance"][...], (padded_high - padded_wide)[:, :rows])
-    level = exact(t["level_flux"][...], balanced) + exact(t["level_jump"][...], jump_narrow)
-    level = level + exact(t["level_wide"][...], joined[:, :rows])
+    balanced = close(t["balance"][...], (padded_high - padded_wide)[:, :rows])
+    level = close(t["level_flux"][...], balanced) + close(t["level_jump"][...], jump_narrow)
+    level = level + close(t["level_wide"][...], joined[:, :rows])
     flux_narrow = jnp.where(row_zero & (own_mode == 0) & holds_steady, balanced, flux_narrow)
     rest = level[:, : LANES - 2 * rows]
     return jnp.concatenate([padded_wide, padded_high, flux_narrow, up(flux_narrow, count), rest], axis=1)

time: 68.8 us -> 68.4 us (level)
  no operation moved by 1% of the time
where the time goes in v7:
time: 68.4 us; the launch traced here: 68.2 us
  Pallas kernels  68.2 us (100%)
    pallas_call x1, Pallas kernels, forward_exchange(): pl.pallas_call(functools.partial(forward_exchange_kernel, steps, groups,...  55.2 us
    pallas_call x1, Pallas kernels, inverse(): pl.pallas_call(functools.partial(inverse_kernel, groups), grid=(steps + g...  13 us

profile of v7, /device:TPU:1, one launch (start us, length us, event | category | flops | bytes accessed | tf_op | source)
XLA Modules:
  0.0 68.2 jit_solution(7928705059289742911)
XLA Ops:
  0.0 55.2 %shard_map.361 = (f32[96,48,256]{2,1,0:T(8,128)}, f32[2,96,256]{2,1,0:T(8,128)}, f32[2,48,256]{2,1,0:T(8,128)}, f32[8,256]{1,0:T(8,128)}) custom-call(f32[48,96,256]{2,1,0:T(8,128)} %refs_0_.1, f32[48,96,256]{2,1,0:T(8,128)} %refs_1_.1, f32[48,96,256]{2,1,0:T(8,128)} %refs_2_.1, bf16[256,256]{1,0:T(8,128)(2,1)} %constant.81.clone.refs_3_, ...), custom_call_target="tpu_custom_call" | custom-call | tf_op jit(solution)/shard_map/pallas_call | solution.py:584
  55.2 13.0 %shard_map.362 = f32[48,96,256]{2,1,0:T(8,128)} custom-call(f32[96,48,256]{2,1,0:T(8,128)} %get-tuple-element.9.spectrum_ref, f32[2,96,256]{2,1,0:T(8,128)} %get-tuple-element.10.wide_ref, f32[2,48,256]{2,1,0:T(8,128)} %get-tuple-element.11.narrow_ref, f32[8,256]{1,0:T(8,128)} %get-tuple-element.12.level_ref, ...), custom_call_target="tpu_custom_call" | custom-call | tf_op jit(solution)/shard_map/pallas_call | solution.py:630
